TPU v7x, 512 devices: a whole 4x4x16 slice. The times are simulated.
512 devices in a mesh: group: 4 (over z_lo), tile: 128 (over x, z_hi, y, core).
Axes of the slice: x: 4, y: 4, z: 16 (z_hi: 4, z_lo: 4; z = z_hi * 4 + z_lo), core: 2. Of those that a mesh axis runs over, the one named last changes fastest.
Arguments:
- potential: float32 [64, 131072], P('group', 'tile'), may hold values from -6 to 6
- species_inputs: bfloat16 [7, 64, 131072], P(None, 'group', 'tile'), may hold values from -6 to 6
- diffusion: float32 [4, 131072], P(None, 'tile'), may hold values from 0.02 to 0.2
- neighbours: int32 [4, 131072], P(None, 'tile'), may hold values from 0 to 1535, as said below
- sunlit_column_index: int32 [4, 128, 256], P('group', 'tile'), may hold values from 0 to 255, each once within a row
- day_count: int32 [4, 128], P('group', 'tile'), may hold values from 0 to 256, as said below
- zenith: bfloat16 [4, 128, 256], P('group', 'tile'), may hold values from 0.099609375 to 1
- lw_first: bfloat16 [8, 64], replicated, may hold values from -2 to 2
- lw_bias: float32 [64], replicated, may hold values from -3 to 3
- lw_second: bfloat16 [64, 64], replicated, may hold values from -0.75 to 0.75
- lw_depth: bfloat16 [64, 256], replicated, may hold values from -0.75 to 0.75
- lw_fraction: bfloat16 [64, 256], replicated, may hold values from -0.75 to 0.75
- sw_first: bfloat16 [8, 64], replicated, may hold values from -2 to 2
- sw_bias: float32 [64], replicated, may hold values from -3 to 3
- sw_second: bfloat16 [64, 64], replicated, may hold values from -0.75 to 0.75
- sw_depth: bfloat16 [64, 224], replicated, may hold values from -0.75 to 0.75
- solar_flux: float32 [224], replicated, may hold values from 0.5 to 2
Outputs:
- evolved: float32 [64, 131072], P('group', 'tile')
Inputs may be any that keep to these rules, and one draw needn't show every extreme that they name: neighbours[k, c] - 256 - (c mod 1024) is a nonzero offset between -256 and 256. `sunlit_column_index`: each list [g, t, :] is a permutation of 0 .. 255. day_count[g, 2 i] + day_count[g, 2 i + 1] = 256 for every g and i.
All inputs are finite; a program needn't handle non-finite values.
Results may differ from a plain program's by a relative error of at most 0.0003.
Values may be sent and summed in bfloat16 or wider, within the bound.
A program may use at most 128 MiB of HBM per device.

v0:
```python
import jax
import jax.numpy as jnp
from jax import lax
from jax.sharding import PartitionSpec as P

COL_DEV = 256
NB = 4
HW = 256


depth_scale = 0.1
heat_scale = 12.0


def extended(cells, sides, width):
    for axis, dim in sides:
        count = lax.axis_size(axis)
        head = lax.slice_in_dim(cells, 0, width, axis=dim)
        tail = lax.slice_in_dim(cells, cells.shape[dim] - width, cells.shape[dim], axis=dim)
        cells = jnp.concatenate(
            [
                lax.ppermute(tail, axis, [(i, (i + 1) % count) for i in range(count)]),
                cells,
                lax.ppermute(head, axis, [((i + 1) % count, i) for i in range(count)]),
            ],
            axis=dim,
        )
    return cells


def in_blocks(value, dim, peers):
    dims = value.shape
    blocks = value.reshape(*dims[:dim], peers, dims[dim] // peers, *dims[dim + 1 :])
    return jnp.moveaxis(blocks, dim, 0)


def edges_of(length, count):
    unit = 8 if length >= 8 * count else 1
    return [length // unit * k // count * unit for k in range(1, count)]


def laid_out(blocks, dim):
    blocks = jnp.moveaxis(blocks, 0, dim)
    dims = blocks.shape
    return blocks.reshape(*dims[:dim], dims[dim] * dims[dim + 1], *dims[dim + 2 :])


def several_exchanges(value, axis, pieces, split_dim, concat_dim):
    blocks = in_blocks(value, split_dim, lax.axis_size(axis))
    split_at = max(range(1, max(2, blocks.ndim - 1)), key=lambda d: blocks.shape[d])
    finished = []
    for slab in jnp.split(blocks, edges_of(blocks.shape[split_at], pieces), axis=split_at):
        if slab.size:
            finished.append(lax.all_to_all(slab, axis, split_axis=0, concat_axis=0, tiled=True))
    return laid_out(jnp.concatenate(finished, axis=split_at), concat_dim)


def swapped(value, axis, stride):
    return lax.ppermute(value, axis, [(i, i ^ 1 << stride) for i in range(lax.axis_size(axis))])


def tendency(framed, base_at, offsets, weights, lower_at):
    span_cols = offsets.shape[1]
    centre = lower_at - base_at + jnp.arange(span_cols, dtype=jnp.int32)
    middle = lax.slice_in_dim(framed, lower_at - base_at, lower_at - base_at + span_cols, axis=1)
    outcome_state = jnp.zeros_like(middle)
    for branch in range(offsets.shape[0]):
        nearby = jnp.take(framed, centre + offsets[branch], axis=1)
        outcome_state = outcome_state + weights[branch] * (nearby - middle)
    return outcome_state


def windowed(table, lower_at, span_cols):
    return lax.slice_in_dim(table, lower_at, lower_at + span_cols, axis=1)


def hidden_layers(inputs, w_first, bias, w_second):
    flat_in = inputs.reshape(inputs.shape[0], -1)
    layer_one = jax.nn.silu(
        jnp.dot(w_first.T, flat_in, preferred_element_type=jnp.float32) + bias[:, None]
    ).astype(jnp.bfloat16)
    return jax.nn.silu(jnp.dot(w_second.T, layer_one, preferred_element_type=jnp.float32)).astype(
        jnp.bfloat16
    )


def longwave(inputs, weights):
    w_first, bias, w_second, w_depth, w_fraction = weights
    vertical_levels, col_count = (inputs.shape[1], inputs.shape[2])
    hidden = hidden_layers(inputs, w_first, bias, w_second)
    depth = depth_scale * jax.nn.softplus(
        jnp.dot(w_depth.T, hidden, preferred_element_type=jnp.float32)
    ).reshape(-1, vertical_levels, col_count)
    fraction = jax.nn.softplus(
        jnp.dot(w_fraction.T, hidden, preferred_element_type=jnp.float32)
    ).reshape(-1, vertical_levels, col_count)
    above = jnp.cumsum(depth, axis=1) - depth
    planck = jnp.exp(0.25 * inputs[0].astype(jnp.float32))
    emitted = jnp.sum(fraction * (1.0 - jnp.exp(-depth)) * jnp.exp(-above), axis=0)
    return -(heat_scale / depth.shape[0]) * planck * emitted


def shortwave(inputs, cosine, weights):
    w_first, bias, w_second, w_depth, solar_flux = weights
    vertical_levels, col_count = (inputs.shape[1], inputs.shape[2])
    hidden = hidden_layers(inputs, w_first, bias, w_second)
    depth = depth_scale * jax.nn.softplus(
        jnp.dot(w_depth.T, hidden, preferred_element_type=jnp.float32)
    ).reshape(-1, vertical_levels, col_count)
    above = jnp.cumsum(depth, axis=1) - depth
    slant = 1.0 / cosine
    beam = (
        solar_flux[:, None, None]
        * cosine
        * jnp.exp(-above * slant)
        * (1.0 - jnp.exp(-depth * slant))
    )
    return heat_scale / depth.shape[0] * jnp.sum(beam, axis=0)


def blockwise(kernel, inputs, cosine, weights):
    span_cols = inputs.shape[2]
    block_cols = 128

    def one_block(begin_at):
        part_in = lax.dynamic_slice_in_dim(inputs, begin_at, block_cols, 2)
        if cosine is None:
            return kernel(part_in, weights)
        return kernel(part_in, cosine, weights)

    starts = jnp.arange(span_cols // block_cols, dtype=jnp.int32) * block_cols
    stacked = lax.map(one_block, starts)
    return jnp.transpose(stacked, (1, 0, 2)).reshape(stacked.shape[1], span_cols)


def per_device(
    potential,
    species_inputs,
    diffusion,
    neighbours,
    sunlit_column_index,
    day_count,
    zenith,
    lw_first,
    lw_bias,
    lw_second,
    lw_depth,
    lw_fraction,
    sw_first,
    sw_bias,
    sw_second,
    sw_depth,
    solar_flux,
):
    slab_rows = potential.shape[0]
    tile_cols = potential.shape[1]
    positions = jnp.arange(tile_cols, dtype=jnp.int32)
    offsets = neighbours - HW - positions[None, :]
    precise = lax.Precision.HIGHEST
    stacked = jnp.concatenate([potential, diffusion, offsets.astype(jnp.float32)], axis=0)
    framed = extended(stacked, (("tile", 1),), 3 * HW)
    field_ext = framed[:slab_rows]
    weights_ext = framed[slab_rows : slab_rows + NB]
    offsets_ext = framed[slab_rows + NB :].astype(jnp.int32)
    span_one = tile_cols + 4 * HW
    span_two = tile_cols + 2 * HW
    first = windowed(field_ext, HW, span_one) + tendency(
        field_ext, 0, windowed(offsets_ext, HW, span_one), windowed(weights_ext, HW, span_one), HW
    )
    second = 0.75 * windowed(field_ext, 2 * HW, span_two) + 0.25 * (
        windowed(first, HW, span_two)
        + tendency(
            first,
            HW,
            windowed(offsets_ext, 2 * HW, span_two),
            windowed(weights_ext, 2 * HW, span_two),
            2 * HW,
        )
    )
    tertile_portion = windowed(field_ext, 3 * HW, tile_cols) / 3.0 + 2.0 / 3.0 * (
        windowed(second, HW, tile_cols)
        + tendency(
            second,
            2 * HW,
            windowed(offsets_ext, 3 * HW, tile_cols),
            windowed(weights_ext, 3 * HW, tile_cols),
            3 * HW,
        )
    )
    kinetic_warmth_field = tertile_portion.astype(jnp.bfloat16)[None]
    columns = several_exchanges(
        jnp.concatenate([kinetic_warmth_field, species_inputs], axis=0), "group", 2, 2, 1
    )
    long_weights = (lw_first, lw_bias, lw_second, lw_depth, lw_fraction)
    short_weights = (sw_first, sw_bias, sw_second, sw_depth, solar_flux)
    zenith_cosine_halves = zenith[0, 0]
    listing = sunlit_column_index[0, 0]
    daylit_count = day_count[0, 0]
    profile_labels = jnp.arange(COL_DEV, dtype=jnp.int32)
    half_column_count = COL_DEV // 2
    slot_ids = jnp.arange(half_column_count, dtype=jnp.int32)
    kept = (
        (listing[:half_column_count][None, :] == profile_labels[:, None])
        & (slot_ids[None, :] < daylit_count)
    ).astype(jnp.bfloat16)
    sent = (
        (listing[half_column_count:][None, :] == profile_labels[:, None])
        & (slot_ids[None, :] + half_column_count < daylit_count)
    ).astype(jnp.bfloat16)
    placed = (slot_ids[None, :] - daylit_count == slot_ids[:, None]).astype(jnp.bfloat16)
    outgoing = jnp.dot(columns, sent, preferred_element_type=jnp.float32).astype(jnp.bfloat16)
    out_cosine = jnp.dot(zenith_cosine_halves, sent, preferred_element_type=jnp.float32).astype(
        jnp.bfloat16
    )
    incoming, in_cosine = swapped((outgoing, out_cosine), "tile", 0)
    work_cols = (
        jnp.dot(columns, kept, preferred_element_type=jnp.float32)
        + jnp.dot(incoming, placed, preferred_element_type=jnp.float32)
    ).astype(jnp.bfloat16)
    work_cosine = jnp.dot(zenith_cosine_halves, kept, preferred_element_type=jnp.float32) + jnp.dot(
        in_cosine, placed, preferred_element_type=jnp.float32
    )
    longwave_heating_rate = blockwise(longwave, columns, None, long_weights)
    work_heat = blockwise(shortwave, work_cols, work_cosine, short_weights)
    back_heat = jnp.dot(work_heat, placed.astype(jnp.float32).T, precision=precise)
    returned = swapped(back_heat, "tile", 0)
    short_heat = jnp.dot(work_heat, kept.astype(jnp.float32).T, precision=precise) + jnp.dot(
        returned, sent.astype(jnp.float32).T, precision=precise
    )
    heating = longwave_heating_rate + short_heat
    slab_heat = lax.all_to_all(heating, "group", split_axis=0, concat_axis=1, tiled=True)
    closing_snapshot = extended(tertile_portion, (("tile", 1),), HW)
    return tertile_portion + tendency(closing_snapshot, 0, offsets, diffusion, HW) + slab_heat


def solution(mesh):
    return jax.shard_map(
        per_device,
        mesh=mesh,
        in_specs=(
            P("group", "tile"),
            P(None, "group", "tile"),
            P(None, "tile"),
            P(None, "tile"),
            P("group", "tile", None),
            P("group", "tile"),
            P("group", "tile", None),
            P(),
            P(),
            P(),
            P(),
            P(),
            P(),
            P(),
            P(),
            P(),
            P(),
        ),
        out_specs=P("group", "tile"),
        check_vma=False,
    )
```

profile of v0, /device:TPU:1, one launch (start us, length us, event | category | flops | bytes accessed | tf_op | source)
XLA Modules:
  0.0 236.9 jit_solution(9991204391452528445)
XLA Ops:
  0.0 0.7 slice_bitcast_fusion
  1.4 1.4 fusion.29
  2.8 8.7 %collective-permute-start.4 = (bf16[128]{0:T(256)(128)(2,1)}, bf16[128]{0:T(256)(128)(2,1)}, u32[]{:S(2)}, u32[]{:S(2)}) collective-permute-start(bf16[128]{0:T(256)(128)(2,1)} %fusion.29), channel_id=1, source_target_pairs={{0,1},{1,0},{2,3},{3,2},{4,5},{5,4},{6,7},{7,6},{8,9},{9,8},{10,11... | collective-permute-start | bytes 776 | tf_op jit(solution)/shard_map/ppermute | solution.py:59
  11.5 0.7 iota_subtract_fusion
  12.2 0.9 pad_maximum_fusion.1
  13.1 1.9 collective-permute-start.1
  15.1 3.6 %collective-permute-start = (f32[24,768]{1,0:T(8,128)S(1)}, f32[24,768]{1,0:T(8,128)S(1)}, u32[]{:S(2)}, u32[]{:S(2)}) collective-permute-start(f32[24,768]{1,0:T(8,128)S(1)} %get-tuple-element.115), channel_id=1, source_target_pairs={{0,1},{1,2},{2,3},{3,4},{4,5},{5,6},{6,7},{7,8},{8,9},{9,10},{10,1... | collective-permute-start | bytes 221192 | tf_op jit(solution)/shard_map/ppermute | solution.py:22
  18.7 0.9 fusion.133
  23.8 1.1 concatenate.24
  24.9 1.4 convolution_bitcast_fusion.6
  26.9 1.0 collective-permute-done
  28.0 0.9 pad_maximum_fusion
  29.6 0.6 compare_and_fusion.6
  30.2 0.6 compare_select_fusion.3
  32.6 0.6 compare_and_fusion.12
  36.0 5.5 %gather_fusion.3 = f32[2048,16]{1,0:T(8,128)S(1)} fusion(f32[16,2560]{0,1:T(8,128)S(1)} %copy.195, s32[2048]{0:T(1024)S(1)} %fusion.109), kind=kCustom, calls=%fused_computation.5.clone | custom fusion | bytes 270336 | tf_op jit(solution)/shard_map/jit(_take)/gather | solution.py:68
  41.8 5.5 %gather_fusion.2 = f32[2048,16]{1,0:T(8,128)S(1)} fusion(f32[16,2560]{0,1:T(8,128)S(1)} %copy.195, s32[2048]{0:T(1024)S(1)} %fusion.108), kind=kCustom, calls=%fused_computation.4.clone | custom fusion | bytes 270336 | tf_op jit(solution)/shard_map/jit(_take)/gather | solution.py:68
  47.6 5.5 %gather_fusion.1 = f32[2048,16]{1,0:T(8,128)S(1)} fusion(f32[16,2560]{0,1:T(8,128)S(1)} %copy.195, s32[2048]{0:T(1024)S(1)} %fusion.107), kind=kCustom, calls=%fused_computation.3.clone | custom fusion | bytes 270336 | tf_op jit(solution)/shard_map/jit(_take)/gather | solution.py:68
  53.4 5.5 %gather_fusion = f32[2048,16]{1,0:T(8,128)S(1)} fusion(f32[16,2560]{0,1:T(8,128)S(1)} %copy.195, s32[2048]{0:T(1024)S(1)} %fusion.106), kind=kCustom, calls=%fused_computation.clone | custom fusion | bytes 270336 | tf_op jit(solution)/shard_map/jit(_take)/gather | solution.py:68
  59.2 0.8 fusion.35
  60.5 0.7 pad_clamp_fusion
  61.2 2.6 %gather_fusion.7 = f32[1536,16]{1,0:T(8,128)S(1)} fusion(f32[16,2048]{0,1:T(8,128)S(1)} %copy.163, s32[2048]{0:T(1024)S(1)} %pad_clamp_fusion), kind=kCustom, calls=%fused_computation.8.clone | custom fusion | bytes 202752 | tf_op jit(solution)/shard_map/jit(_take)/gather | solution.py:68
  64.0 2.6 %gather_fusion.6 = f32[1536,16]{1,0:T(8,128)S(1)} fusion(f32[16,2048]{0,1:T(8,128)S(1)} %copy.163, s32[2048]{0:T(1024)S(1)} %pad_clamp_fusion.1), kind=kCustom, calls=%fused_computation.7.clone | custom fusion | bytes 202752 | tf_op jit(solution)/shard_map/jit(_take)/gather | solution.py:68
  67.0 2.6 %gather_fusion.5 = f32[1536,16]{1,0:T(8,128)S(1)} fusion(f32[16,2048]{0,1:T(8,128)S(1)} %copy.163, s32[2048]{0:T(1024)S(1)} %pad_clamp_fusion.2), kind=kCustom, calls=%fused_computation.6.clone | custom fusion | bytes 202752 | tf_op jit(solution)/shard_map/jit(_take)/gather | solution.py:68
  69.8 2.6 %gather_fusion.4 = f32[1536,16]{1,0:T(8,128)S(1)} fusion(f32[16,2048]{0,1:T(8,128)S(1)} %copy.163, s32[2048]{0:T(1024)S(1)} %pad_clamp_fusion.3), kind=kCustom, calls=%fused_computation.1.clone | custom fusion | bytes 202752 | tf_op jit(solution)/shard_map/jit(_take)/gather | solution.py:68
  73.2 2.8 %gather_fusion.11 = f32[1024,16]{1,0:T(8,128)S(1)} fusion(f32[16,1536]{0,1:T(8,128)S(1)} %copy.171, s32[1024]{0:T(1024)S(1)} %copy-done.22), kind=kCustom, calls=%fused_computation.11.clone | custom fusion | bytes 135168 | tf_op jit(solution)/shard_map/jit(_take)/gather | solution.py:68
  76.2 2.8 %gather_fusion.10 = f32[1024,16]{1,0:T(8,128)S(1)} fusion(f32[16,1536]{0,1:T(8,128)S(1)} %copy.171, s32[1024]{0:T(1024)S(1)} %copy-done.23), kind=kCustom, calls=%fused_computation.10.clone | custom fusion | bytes 135168 | tf_op jit(solution)/shard_map/jit(_take)/gather | solution.py:68
  79.2 2.8 %gather_fusion.9 = f32[1024,16]{1,0:T(8,128)S(1)} fusion(f32[16,1536]{0,1:T(8,128)S(1)} %copy.171, s32[1024]{0:T(1024)S(1)} %copy-done.21), kind=kCustom, calls=%fused_computation.9.clone | custom fusion | bytes 135168 | tf_op jit(solution)/shard_map/jit(_take)/gather | solution.py:68
  82.2 2.8 %gather_fusion.8 = f32[1024,16]{1,0:T(8,128)S(1)} fusion(f32[16,1536]{0,1:T(8,128)S(1)} %copy.171, s32[1024]{0:T(1024)S(1)} %copy-done.24), kind=kCustom, calls=%fused_computation.2.clone | custom fusion | bytes 135168 | tf_op jit(solution)/shard_map/jit(_take)/gather | solution.py:68
  85.6 0.7 copy.188
  86.3 3.3 %all-to-all-start.1 = ((bf16[4,8,8,256]{3,2,1,0:T(8,128)(2,1)}), bf16[4,8,8,256]{3,2,1,0:T(8,128)(2,1)S(1)}, u32[]{:S(2)}, u32[]{:S(2)}) async-start(bf16[4,8,8,256]{3,2,1,0:T(8,128)(2,1)} %copy.188), calls=%async_computation.1 | async-start | bytes 262144 | tf_op jit(solution)/shard_map/all_to_all | solution.py:54
  89.6 0.8 broadcast_divide_fusion
  90.4 0.8 broadcast_multiply_fusion
  91.2 0.7 copy.187
  91.9 2.5 %all-to-all-done.1 = bf16[4,8,8,256]{3,2,1,0:T(8,128)(2,1)S(1)} async-done(((bf16[4,8,8,256]{3,2,1,0:T(8,128)(2,1)}), bf16[4,8,8,256]{3,2,1,0:T(8,128)(2,1)S(1)}, u32[]{:S(2)}, u32[]{:S(2)}) %all-to-all-start.1) | async-done | bytes 131104 | tf_op jit(solution)/shard_map/all_to_all | solution.py:54
  94.4 3.3 %all-to-all-start = ((bf16[4,8,8,256]{3,2,1,0:T(8,128)(2,1)}), bf16[4,8,8,256]{3,2,1,0:T(8,128)(2,1)S(1)}, u32[]{:S(2)}, u32[]{:S(2)}) async-start(bf16[4,8,8,256]{3,2,1,0:T(8,128)(2,1)} %copy.187), calls=%async_computation | async-start | bytes 262144 | tf_op jit(solution)/shard_map/all_to_all | solution.py:54
  98.3 0.6 fusion.129
  98.9 16.1 %collective-permute-start.3 = (f32[16,256]{1,0:T(8,128)}, f32[16,256]{1,0:T(8,128)}, u32[]{:S(2)}, u32[]{:S(2)}) collective-permute-start(f32[16,256]{1,0:T(8,128)} %get-tuple-element.118), channel_id=1, source_target_pairs={{1,0},{2,1},{3,2},{4,3},{5,4},{6,5},{7,6},{8,7},{9,8},{10,9},{11,1... | collective-permute-start | bytes 49160 | tf_op jit(solution)/shard_map/ppermute | solution.py:24
  115.0 1.9 collective-permute-start.2
  117.3 5.6 %collective-permute-start.5 = (bf16[8,64,128]{2,1,0:T(8,128)(2,1)S(1)}, bf16[8,64,128]{2,1,0:T(8,128)(2,1)S(1)}, u32[]{:S(2)}, u32[]{:S(2)}) collective-permute-start(bf16[8,64,128]{2,1,0:T(8,128)(2,1)S(1)} %convolution_convert_fusion), channel_id=1, source_target_pairs={{0,1},{1,0},{2,3},{3,2},{4,5},{5,4},{6,7},{7,6},{8,9},{9,8},{10,11... | collective-permute-start | bytes 393224 | tf_op jit(solution)/shard_map/ppermute | solution.py:59
  123.0 61.7 %while.2 = (s32[]{:T(128)}, f32[2,64,128]{2,1,0:T(8,128)S(1)}, s32[2]{0:T(128)S(1)}, bf16[8,64,256]{2,1,0:T(8,128)(2,1)S(1)}, bf16[8,64]{1,0:T(8,128)(2,1)S(1)},...) while((s32[]{:T(128)}, f32[2,64,128]{2,1,0:T(8,128)S(1)}, ...), condition=%wide.region_3.7_spmd, body=%wide.region_0.6_spmd.sunk | while | flops 792223744 | bytes 45671864 | solution.py:132
  125.6 1.5 multiply_convert_fusion.5
  127.1 8.5 %fusion.177 = f32[256,8192]{1,0:T(8,128)} fusion(bf16[64,8192]{1,0:T(8,128)(2,1)S(1)} %multiply_convert_fusion.5, bf16[64,256]{1,0:T(8,128)(2,1)S(1)} %get-tuple-element.248), kind=kOutput, calls=%fused_computation.26.clone.1 | convolution fusion | flops 283115520 | bytes 9469952 | tf_op jit(solution)/shard_map/while/body/eval_jaxpr/dot_general | solution.py:92
  135.6 7.2 %fusion.178 = f32[256,64,128]{2,0,1:T(8,128)} fusion(f32[256,8192]{1,0:T(8,128)} %fusion.177), kind=kOutput, calls=%fused_computation.30.clone.1 | output fusion | flops 132120576 | bytes 16777216 | tf_op jit(solution)/shard_map/while/body/eval_jaxpr/jit(cumsum)/reduce_window_sum | solution.py:97
  142.9 10.7 %fusion.179 = f32[8192]{0:T(1024)S(1)} fusion(f32[256,8192]{1,0:T(8,128)} %fusion.177, bf16[64,8192]{1,0:T(8,128)(2,1)S(1)} %multiply_convert_fusion.5, bf16[64,256]{1,0:T(8,128)(2,1)S(1)} %get-tuple-element.247, f32[256,64,128]{2,0,1:T(8,128)} %fusion.178), kind=kOutput, calls=%fused_computation.25.clone.1 | convolution fusion | flops 295690240 | bytes 17891328 | tf_op jit(solution)/shard_map/while/body/eval_jaxpr/dot_general | solution.py:95
  156.4 1.5 multiply_convert_fusion.5
  157.9 8.5 %fusion.177 = f32[256,8192]{1,0:T(8,128)} fusion(bf16[64,8192]{1,0:T(8,128)(2,1)S(1)} %multiply_convert_fusion.5, bf16[64,256]{1,0:T(8,128)(2,1)S(1)} %get-tuple-element.248), kind=kOutput, calls=%fused_computation.26.clone.1 | convolution fusion | flops 283115520 | bytes 9469952 | tf_op jit(solution)/shard_map/while/body/eval_jaxpr/dot_general | solution.py:92
  166.4 7.2 %fusion.178 = f32[256,64,128]{2,0,1:T(8,128)} fusion(f32[256,8192]{1,0:T(8,128)} %fusion.177), kind=kOutput, calls=%fused_computation.30.clone.1 | output fusion | flops 132120576 | bytes 16777216 | tf_op jit(solution)/shard_map/while/body/eval_jaxpr/jit(cumsum)/reduce_window_sum | solution.py:97
  173.6 10.7 %fusion.179 = f32[8192]{0:T(1024)S(1)} fusion(f32[256,8192]{1,0:T(8,128)} %fusion.177, bf16[64,8192]{1,0:T(8,128)(2,1)S(1)} %multiply_convert_fusion.5, bf16[64,256]{1,0:T(8,128)(2,1)S(1)} %get-tuple-element.247, f32[256,64,128]{2,0,1:T(8,128)} %fusion.178), kind=kOutput, calls=%fused_computation.25.clone.1 | convolution fusion | flops 295690240 | bytes 17891328 | tf_op jit(solution)/shard_map/while/body/eval_jaxpr/dot_general | solution.py:95
  185.2 0.8 multiply_convert_fusion.3
  186.0 8.2 %fusion.17 = f32[224,8192]{1,0:T(8,128)} fusion(bf16[64,224]{1,0:T(8,128)(2,1)S(1)} %copy-done, bf16[64,8192]{1,0:T(8,128)(2,1)S(1)} %multiply_convert_fusion.3, bf16[64,64]{1,0:T(8,128)(2,1)S(1)} %copy-done.52), kind=kOutput, calls=%fused_computation.46 | convolution fusion | flops 317456384 | bytes 8425472 | tf_op jit(solution)/shard_map/while/body/eval_jaxpr/dot_general | solution.py:108
  194.2 6.5 %fusion.23 = f32[224,64,128]{2,0,1:T(8,128)} fusion(f32[224,8192]{1,0:T(8,128)} %fusion.17), kind=kOutput, calls=%fused_computation.54 | output fusion | flops 115605504 | bytes 14680064 | tf_op jit(solution)/shard_map/while/body/eval_jaxpr/jit(cumsum)/reduce_window_sum | solution.py:110
  201.2 2.6 %copy-done.1 = f32[224,8192]{1,0:T(8,128)S(1)} copy-done((f32[224,8192]{1,0:T(8,128)S(1)}, f32[224,8192]{1,0:T(8,128)}, u32[]{:S(2)}) %copy-start.1) | copy-done | bytes 7340056
  203.9 10.5 %fusion.19 = f32[8192]{0:T(1024)S(1)} fusion(f32[28,8,64,128]{3,2,1,0:T(8,128)S(1)} %bitcast.356, f32[224,8192]{1,0:T(8,128)S(1)} %copy-done.1, f32[8192]{0:T(1024)S(1)} %copy-done.7, f32[224,64,128]{2,0,1:T(8,128)} %fusion.23), kind=kLoop, calls=%fused_computation.49 | loop fusion | flops 16506880 | bytes 22085632 | tf_op jit(solution)/shard_map/while/body/eval_jaxpr/reduce_sum | solution.py:118
  214.7 1.9 collective-permute-start.6
  216.8 1.0 collective-permute-done.6
  217.8 0.8 fusion.28
  218.6 4.5 %all-to-all-start.2 = ((f32[4,16,256]{2,1,0:T(8,128)}), f32[4,16,256]{2,1,0:T(8,128)S(1)}, u32[]{:S(2)}, u32[]{:S(2)}) async-start(f32[4,16,256]{2,1,0:T(8,128)} %bitcast.61), calls=%async_computation.2 | async-start | bytes 131072 | tf_op jit(solution)/shard_map/all_to_all | solution.py:231
  223.2 0.7 pad_maximum_fusion.2
  224.2 2.8 %gather_fusion.15 = f32[1024,16]{1,0:T(8,128)S(1)} fusion(f32[16,1536]{0,1:T(8,128)S(1)} %copy.179, s32[1024]{0:T(1024)S(1)} %copy-done.20), kind=kCustom, calls=%fused_computation.15.clone | custom fusion | bytes 135168 | tf_op jit(solution)/shard_map/jit(_take)/gather | solution.py:68
  227.2 2.8 %gather_fusion.14 = f32[1024,16]{1,0:T(8,128)S(1)} fusion(f32[16,1536]{0,1:T(8,128)S(1)} %copy.179, s32[1024]{0:T(1024)S(1)} %copy-done.17), kind=kCustom, calls=%fused_computation.14.clone | custom fusion | bytes 135168 | tf_op jit(solution)/shard_map/jit(_take)/gather | solution.py:68
  230.2 2.8 %gather_fusion.13 = f32[1024,16]{1,0:T(8,128)S(1)} fusion(f32[16,1536]{0,1:T(8,128)S(1)} %copy.179, s32[1024]{0:T(1024)S(1)} %copy-done.19), kind=kCustom, calls=%fused_computation.13.clone | custom fusion | bytes 135168 | tf_op jit(solution)/shard_map/jit(_take)/gather | solution.py:68
  233.2 2.8 %gather_fusion.12 = f32[1024,16]{1,0:T(8,128)S(1)} fusion(f32[16,1536]{0,1:T(8,128)S(1)} %copy.179, s32[1024]{0:T(1024)S(1)} %copy-done.18), kind=kCustom, calls=%fused_computation.12.clone | custom fusion | bytes 135168 | tf_op jit(solution)/shard_map/jit(_take)/gather | solution.py:68
  236.3 0.7 fusion.66
  (203 shorter events, 19.1 us)
Async XLA Ops:
  0.0 186.0 %copy-start = (bf16[64,224]{1,0:T(8,128)(2,1)S(1)}, bf16[64,224]{1,0:T(8,128)(2,1)}, u32[]{:S(2)}) copy-start(bf16[64,224]{1,0:T(8,128)(2,1)} %param.40) | copy-start | bytes 86020
  0.0 59.2 %copy-start.3 = (f32[4,1024]{1,0:T(4,128)S(1)}, f32[4,1024]{1,0:T(4,128)}, u32[]{:S(2)}) copy-start(f32[4,1024]{1,0:T(4,128)} %param.27) | copy-start | bytes 49156
  0.0 59.2 %copy-start.2 = (f32[16,1024]{1,0:T(8,128)S(1)}, f32[16,1024]{1,0:T(8,128)}, u32[]{:S(2)}) copy-start(f32[16,1024]{1,0:T(8,128)} %param.25) | copy-start | bytes 196612
  0.7 11.5 %copy-start.29 = (s32[128]{0:T(128)}, s32[128]{0:T(128)S(1)}, u32[]{:S(2)}) copy-start(s32[128]{0:T(128)S(1)} %get-tuple-element.137) | copy-start | bytes 1540
  0.7 30.7 %copy-start.32 = (s32[128]{0:T(128)}, s32[128]{0:T(128)S(1)}, u32[]{:S(2)}) copy-start(s32[128]{0:T(128)S(1)} %get-tuple-element.138) | copy-start | bytes 1540
  2.8 86.9 %collective-permute-start.4 = (bf16[128]{0:T(256)(128)(2,1)}, bf16[128]{0:T(256)(128)(2,1)}, u32[]{:S(2)}, u32[]{:S(2)}) collective-permute-start(bf16[128]{0:T(256)(128)(2,1)} %fusion.29), channel_id=1, source_target_pairs={{0,1},{1,0},{2,3},{3,2},{4,5},{5,4},{6,7},{7,6},{8,9},{9,8},{10,11... | collective-permute-start | bytes 776 | tf_op jit(solution)/shard_map/ppermute | solution.py:59
  13.1 13.8 %collective-permute-start.1 = (f32[24,768]{1,0:T(8,128)S(1)}, f32[24,768]{1,0:T(8,128)S(1)}, u32[]{:S(2)}, u32[]{:S(2)}) collective-permute-start(f32[24,768]{1,0:T(8,128)S(1)} %get-tuple-element.116), channel_id=1, source_target_pairs={{1,0},{2,1},{3,2},{4,3},{5,4},{6,5},{7,6},{8,7},{9,8},{10,9},{11,1... | collective-permute-start | bytes 221192 | tf_op jit(solution)/shard_map/ppermute | solution.py:24
  15.1 12.9 %collective-permute-start = (f32[24,768]{1,0:T(8,128)S(1)}, f32[24,768]{1,0:T(8,128)S(1)}, u32[]{:S(2)}, u32[]{:S(2)}) collective-permute-start(f32[24,768]{1,0:T(8,128)S(1)} %get-tuple-element.115), channel_id=1, source_target_pairs={{0,1},{1,2},{2,3},{3,4},{4,5},{5,6},{6,7},{7,8},{8,9},{9,10},{10,1... | collective-permute-start | bytes 221192 | tf_op jit(solution)/shard_map/ppermute | solution.py:22
  19.6 65.5 %copy-start.9 = (f32[1,1024]{1,0:T(1,128)}, f32[1,1024]{1,0:T(1,128)S(1)}, u32[]{:S(2)}) copy-start(f32[1,1024]{1,0:T(1,128)S(1)} %get-tuple-element.133) | copy-start | bytes 12292
  19.6 65.5 %copy-start.11 = (f32[1,1024]{1,0:T(1,128)}, f32[1,1024]{1,0:T(1,128)S(1)}, u32[]{:S(2)}) copy-start(f32[1,1024]{1,0:T(1,128)S(1)} %get-tuple-element.134) | copy-start | bytes 12292
  19.6 65.5 %copy-start.13 = (f32[1,1024]{1,0:T(1,128)}, f32[1,1024]{1,0:T(1,128)S(1)}, u32[]{:S(2)}) copy-start(f32[1,1024]{1,0:T(1,128)S(1)} %get-tuple-element.135) | copy-start | bytes 12292
  19.6 65.5 %copy-start.15 = (f32[1,1024]{1,0:T(1,128)}, f32[1,1024]{1,0:T(1,128)S(1)}, u32[]{:S(2)}) copy-start(f32[1,1024]{1,0:T(1,128)S(1)} %get-tuple-element.136) | copy-start | bytes 12292
  58.8 14.3 %copy-start.22 = (s32[1024]{0:T(1024)S(1)}, s32[1024]{0:T(1024)}, u32[]{:S(2)}) copy-start(s32[1024]{0:T(1024)} %fusion.113) | copy-start | bytes 12292
  59.2 20.0 %copy-start.21 = (s32[1024]{0:T(1024)S(1)}, s32[1024]{0:T(1024)}, u32[]{:S(2)}) copy-start(s32[1024]{0:T(1024)} %fusion.111) | copy-start | bytes 12292
  60.0 12.7 %copy-start.25 = (pred[1536]{0:T(1024)(128)(4,1)S(1)}, pred[1536]{0:T(1024)(128)(4,1)}, u32[]{:S(2)}) copy-start(pred[1536]{0:T(1024)(128)(4,1)} %get-tuple-element.149) | copy-start | bytes 4612
  60.0 12.7 %copy-start.26 = (pred[1536]{0:T(1024)(128)(4,1)S(1)}, pred[1536]{0:T(1024)(128)(4,1)}, u32[]{:S(2)}) copy-start(pred[1536]{0:T(1024)(128)(4,1)} %get-tuple-element.150) | copy-start | bytes 4612
  60.1 12.7 %copy-start.27 = (pred[1536]{0:T(1024)(128)(4,1)S(1)}, pred[1536]{0:T(1024)(128)(4,1)}, u32[]{:S(2)}) copy-start(pred[1536]{0:T(1024)(128)(4,1)} %get-tuple-element.151) | copy-start | bytes 4612
  60.1 12.7 %copy-start.28 = (pred[1536]{0:T(1024)(128)(4,1)S(1)}, pred[1536]{0:T(1024)(128)(4,1)}, u32[]{:S(2)}) copy-start(pred[1536]{0:T(1024)(128)(4,1)} %get-tuple-element.152) | copy-start | bytes 4612
  60.1 16.1 %copy-start.23 = (s32[1024]{0:T(1024)S(1)}, s32[1024]{0:T(1024)}, u32[]{:S(2)}) copy-start(s32[1024]{0:T(1024)} %fusion.112) | copy-start | bytes 12292
  60.1 22.1 %copy-start.24 = (s32[1024]{0:T(1024)S(1)}, s32[1024]{0:T(1024)}, u32[]{:S(2)}) copy-start(s32[1024]{0:T(1024)} %fusion.110) | copy-start | bytes 12292
  60.4 24.7 %copy-start.38 = (pred[1024]{0:T(1024)(128)(4,1)S(1)}, pred[1024]{0:T(1024)(128)(4,1)}, u32[]{:S(2)}) copy-start(pred[1024]{0:T(1024)(128)(4,1)} %get-tuple-element.153) | copy-start | bytes 3076
  60.4 24.7 %copy-start.39 = (pred[1024]{0:T(1024)(128)(4,1)S(1)}, pred[1024]{0:T(1024)(128)(4,1)}, u32[]{:S(2)}) copy-start(pred[1024]{0:T(1024)(128)(4,1)} %get-tuple-element.154) | copy-start | bytes 3076
  60.5 24.7 %copy-start.40 = (pred[1024]{0:T(1024)(128)(4,1)S(1)}, pred[1024]{0:T(1024)(128)(4,1)}, u32[]{:S(2)}) copy-start(pred[1024]{0:T(1024)(128)(4,1)} %get-tuple-element.155) | copy-start | bytes 3076
  60.5 24.7 %copy-start.41 = (pred[1024]{0:T(1024)(128)(4,1)S(1)}, pred[1024]{0:T(1024)(128)(4,1)}, u32[]{:S(2)}) copy-start(pred[1024]{0:T(1024)(128)(4,1)} %get-tuple-element.156) | copy-start | bytes 3076
  64.0 25.6 %copy-start.45 = (s32[128]{0:T(128)S(1)}, s32[128]{0:T(128)}, u32[]{:S(2)}) copy-start(s32[128]{0:T(128)} %iota_subtract_fusion.1) | copy-start | bytes 1540
  64.0 25.6 %copy-start.58 = (f32[128]{0:T(128)S(1)}, f32[128]{0:T(128)}, u32[]{:S(2)}) copy-start(f32[128]{0:T(128)} %convolution_bitcast_fusion.6) | copy-start | bytes 1540
  64.0 26.4 %copy-start.48 = (f32[224]{0:T(256)S(1)}, f32[224]{0:T(256)}, u32[]{:S(2)}) copy-start(f32[224]{0:T(256)} %param.41) | copy-start | bytes 2692
  66.9 50.2 %copy-start.30 = (s32[128]{0:T(128)S(1)}, s32[128]{0:T(128)}, u32[]{:S(2)}) copy-start(s32[128]{0:T(128)} %copy-done.29) | copy-start | bytes 1540
  66.9 50.2 %copy-start.43 = (pred[128]{0:T(512)(128)(4,1)S(1)}, pred[128]{0:T(512)(128)(4,1)}, u32[]{:S(2)}) copy-start(pred[128]{0:T(512)(128)(4,1)} %copy-done.42) | copy-start | bytes 388
  66.9 56.0 %copy-start.8 = (f32[2,64,128]{2,1,0:T(8,128)S(1)}, f32[2,64,128]{2,1,0:T(8,128)}, u32[]{:S(2)}) copy-start(f32[2,64,128]{2,1,0:T(8,128)} %custom-call.32) | copy-start | bytes 196612
  66.9 55.9 %copy-start.49 = (bf16[64,256]{1,0:T(8,128)(2,1)S(1)}, bf16[64,256]{1,0:T(8,128)(2,1)}, u32[]{:S(2)}) copy-start(bf16[64,256]{1,0:T(8,128)(2,1)} %param.36) | copy-start | bytes 98308
  66.9 55.9 %copy-start.50 = (bf16[64,256]{1,0:T(8,128)(2,1)S(1)}, bf16[64,256]{1,0:T(8,128)(2,1)}, u32[]{:S(2)}) copy-start(bf16[64,256]{1,0:T(8,128)(2,1)} %param.35) | copy-start | bytes 98308
  66.9 55.9 %copy-start.51 = (bf16[64,64]{1,0:T(8,128)(2,1)S(1)}, bf16[64,64]{1,0:T(8,128)(2,1)}, u32[]{:S(2)}) copy-start(bf16[64,64]{1,0:T(8,128)(2,1)} %param.34) | copy-start | bytes 24580
  66.9 55.9 %copy-start.53 = (bf16[8,64]{1,0:T(8,128)(2,1)S(1)}, bf16[8,64]{1,0:T(8,128)(2,1)}, u32[]{:S(2)}) copy-start(bf16[8,64]{1,0:T(8,128)(2,1)} %param.32) | copy-start | bytes 3076
  67.0 55.9 %copy-start.55 = (f32[64]{0:T(128)S(1)}, f32[64]{0:T(128)}, u32[]{:S(2)}) copy-start(f32[64]{0:T(128)} %param.33) | copy-start | bytes 772
  67.0 55.9 %copy-start.57 = (s32[2]{0:T(128)S(1)}, s32[2]{0:T(128)}, u32[]{:S(2)}) copy-start(s32[2]{0:T(128)} %iota_multiply_fusion) | copy-start | bytes 28
  85.3 31.7 %copy-start.4 = (f32[16,1024]{1,0:T(8,128)}, f32[16,1024]{1,0:T(8,128)S(1)}, u32[]{:S(2)}) copy-start(f32[16,1024]{1,0:T(8,128)S(1)} %get-tuple-element.109) | copy-start | bytes 196612
  86.3 8.1 %all-to-all-start.1 = ((bf16[4,8,8,256]{3,2,1,0:T(8,128)(2,1)}), bf16[4,8,8,256]{3,2,1,0:T(8,128)(2,1)S(1)}, u32[]{:S(2)}, u32[]{:S(2)}) async-start(bf16[4,8,8,256]{3,2,1,0:T(8,128)(2,1)} %copy.188), calls=%async_computation.1 | async-start | bytes 262144 | tf_op jit(solution)/shard_map/all_to_all | solution.py:54
  94.4 22.6 %all-to-all-start = ((bf16[4,8,8,256]{3,2,1,0:T(8,128)(2,1)}), bf16[4,8,8,256]{3,2,1,0:T(8,128)(2,1)S(1)}, u32[]{:S(2)}, u32[]{:S(2)}) async-start(bf16[4,8,8,256]{3,2,1,0:T(8,128)(2,1)} %copy.187), calls=%async_computation | async-start | bytes 262144 | tf_op jit(solution)/shard_map/all_to_all | solution.py:54
  98.9 124.3 %collective-permute-start.3 = (f32[16,256]{1,0:T(8,128)}, f32[16,256]{1,0:T(8,128)}, u32[]{:S(2)}, u32[]{:S(2)}) collective-permute-start(f32[16,256]{1,0:T(8,128)} %get-tuple-element.118), channel_id=1, source_target_pairs={{1,0},{2,1},{3,2},{4,3},{5,4},{6,5},{7,6},{8,7},{9,8},{10,9},{11,1... | collective-permute-start | bytes 49160 | tf_op jit(solution)/shard_map/ppermute | solution.py:24
  115.0 108.1 %collective-permute-start.2 = (f32[16,256]{1,0:T(8,128)}, f32[16,256]{1,0:T(8,128)}, u32[]{:S(2)}, u32[]{:S(2)}) collective-permute-start(f32[16,256]{1,0:T(8,128)} %get-tuple-element.117), channel_id=1, source_target_pairs={{0,1},{1,2},{2,3},{3,4},{4,5},{5,6},{6,7},{7,8},{8,9},{9,10},{10,1... | collective-permute-start | bytes 49160 | tf_op jit(solution)/shard_map/ppermute | solution.py:22
  117.3 67.7 %collective-permute-start.5 = (bf16[8,64,128]{2,1,0:T(8,128)(2,1)S(1)}, bf16[8,64,128]{2,1,0:T(8,128)(2,1)S(1)}, u32[]{:S(2)}, u32[]{:S(2)}) collective-permute-start(bf16[8,64,128]{2,1,0:T(8,128)(2,1)S(1)} %convolution_convert_fusion), channel_id=1, source_target_pairs={{0,1},{1,0},{2,3},{3,2},{4,5},{5,4},{6,7},{7,6},{8,9},{9,8},{10,11... | collective-permute-start | bytes 393224 | tf_op jit(solution)/shard_map/ppermute | solution.py:59
  122.9 61.8 %copy-start.33 = (s32[128]{0:T(128)S(1)}, s32[128]{0:T(128)}, u32[]{:S(2)}) copy-start(s32[128]{0:T(128)} %copy-done.32) | copy-start | bytes 1540
  122.9 61.8 %copy-start.47 = (pred[128]{0:T(512)(128)(4,1)S(1)}, pred[128]{0:T(512)(128)(4,1)}, u32[]{:S(2)}) copy-start(pred[128]{0:T(512)(128)(4,1)} %copy-done.46) | copy-start | bytes 388
  122.9 62.2 %copy-start.54 = (bf16[8,64]{1,0:T(8,128)(2,1)S(1)}, bf16[8,64]{1,0:T(8,128)(2,1)}, u32[]{:S(2)}) copy-start(bf16[8,64]{1,0:T(8,128)(2,1)} %param.37) | copy-start | bytes 3076
  122.9 62.2 %copy-start.56 = (f32[64]{0:T(128)S(1)}, f32[64]{0:T(128)}, u32[]{:S(2)}) copy-start(f32[64]{0:T(128)} %param.38) | copy-start | bytes 772
  194.2 6.5 %copy-start.6 = (f32[224,128]{1,0:T(8,128)S(1)}, f32[224,128]{1,0:T(8,128)}, u32[]{:S(2)}) copy-start(f32[224,128]{1,0:T(8,128)} %broadcast_multiply_fusion) | copy-start | bytes 344068
  203.8 14.0 %copy-start.31 = (s32[128]{0:T(128)S(1)}, s32[128]{0:T(128)}, u32[]{:S(2)}) copy-start(s32[128]{0:T(128)} %copy-done.29) | copy-start | bytes 1540
  203.8 14.0 %copy-start.44 = (pred[128]{0:T(512)(128)(4,1)S(1)}, pred[128]{0:T(512)(128)(4,1)}, u32[]{:S(2)}) copy-start(pred[128]{0:T(512)(128)(4,1)} %copy-done.42) | copy-start | bytes 388
  203.8 19.4 %copy-start.5 = (f32[16,1024]{1,0:T(8,128)S(1)}, f32[16,1024]{1,0:T(8,128)}, u32[]{:S(2)}) copy-start(f32[16,1024]{1,0:T(8,128)} %copy-done.4) | copy-start | bytes 196612
  203.8 20.4 %copy-start.20 = (s32[1024]{0:T(1024)S(1)}, s32[1024]{0:T(1024)}, u32[]{:S(2)}) copy-start(s32[1024]{0:T(1024)} %fusion.117) | copy-start | bytes 12292
  203.8 23.4 %copy-start.17 = (s32[1024]{0:T(1024)S(1)}, s32[1024]{0:T(1024)}, u32[]{:S(2)}) copy-start(s32[1024]{0:T(1024)} %fusion.116) | copy-start | bytes 12292
  203.8 26.4 %copy-start.19 = (s32[1024]{0:T(1024)S(1)}, s32[1024]{0:T(1024)}, u32[]{:S(2)}) copy-start(s32[1024]{0:T(1024)} %fusion.115) | copy-start | bytes 12292
  203.8 29.3 %copy-start.18 = (s32[1024]{0:T(1024)S(1)}, s32[1024]{0:T(1024)}, u32[]{:S(2)}) copy-start(s32[1024]{0:T(1024)} %fusion.114) | copy-start | bytes 12292
  203.8 32.3 %copy-start.10 = (f32[1,1024]{1,0:T(1,128)S(1)}, f32[1,1024]{1,0:T(1,128)}, u32[]{:S(2)}) copy-start(f32[1,1024]{1,0:T(1,128)} %copy-done.9) | copy-start | bytes 12292
  203.8 32.3 %copy-start.12 = (f32[1,1024]{1,0:T(1,128)S(1)}, f32[1,1024]{1,0:T(1,128)}, u32[]{:S(2)}) copy-start(f32[1,1024]{1,0:T(1,128)} %copy-done.11) | copy-start | bytes 12292
  203.9 32.3 %copy-start.14 = (f32[1,1024]{1,0:T(1,128)S(1)}, f32[1,1024]{1,0:T(1,128)}, u32[]{:S(2)}) copy-start(f32[1,1024]{1,0:T(1,128)} %copy-done.13) | copy-start | bytes 12292
  203.9 32.3 %copy-start.16 = (f32[1,1024]{1,0:T(1,128)S(1)}, f32[1,1024]{1,0:T(1,128)}, u32[]{:S(2)}) copy-start(f32[1,1024]{1,0:T(1,128)} %copy-done.15) | copy-start | bytes 12292
  203.9 32.3 %copy-start.34 = (pred[1024]{0:T(1024)(128)(4,1)S(1)}, pred[1024]{0:T(1024)(128)(4,1)}, u32[]{:S(2)}) copy-start(pred[1024]{0:T(1024)(128)(4,1)} %get-tuple-element.157) | copy-start | bytes 3076
  203.9 32.3 %copy-start.35 = (pred[1024]{0:T(1024)(128)(4,1)S(1)}, pred[1024]{0:T(1024)(128)(4,1)}, u32[]{:S(2)}) copy-start(pred[1024]{0:T(1024)(128)(4,1)} %get-tuple-element.158) | copy-start | bytes 3076
  203.9 32.3 %copy-start.36 = (pred[1024]{0:T(1024)(128)(4,1)S(1)}, pred[1024]{0:T(1024)(128)(4,1)}, u32[]{:S(2)}) copy-start(pred[1024]{0:T(1024)(128)(4,1)} %get-tuple-element.159) | copy-start | bytes 3076
  203.9 32.3 %copy-start.37 = (pred[1024]{0:T(1024)(128)(4,1)S(1)}, pred[1024]{0:T(1024)(128)(4,1)}, u32[]{:S(2)}) copy-start(pred[1024]{0:T(1024)(128)(4,1)} %get-tuple-element.160) | copy-start | bytes 3076
  214.7 3.1 %collective-permute-start.6 = (f32[64,128]{1,0:T(8,128)S(1)}, f32[64,128]{1,0:T(8,128)S(1)}, u32[]{:S(2)}, u32[]{:S(2)}) collective-permute-start(f32[64,128]{1,0:T(8,128)S(1)} %fusion.82), channel_id=1, source_target_pairs={{0,1},{1,0},{2,3},{3,2},{4,5},{5,4},{6,7},{7,6},{8,9},{9,8},{10,11... | collective-permute-start | bytes 98312 | tf_op jit(solution)/shard_map/ppermute | solution.py:59
  218.6 17.5 %all-to-all-start.2 = ((f32[4,16,256]{2,1,0:T(8,128)}), f32[4,16,256]{2,1,0:T(8,128)S(1)}, u32[]{:S(2)}, u32[]{:S(2)}) async-start(f32[4,16,256]{2,1,0:T(8,128)} %bitcast.61), calls=%async_computation.2 | async-start | bytes 131072 | tf_op jit(solution)/shard_map/all_to_all | solution.py:231
  (5 other events, 11.9 us)
where the time goes:
time: 238 us; the launch traced here: 237 us
  local copies, waits for them, and re-layouts  69.7 us (29%)
  matrix products  55.9 us (23%)
  starting transfers between devices  51 us (21%)
  other arithmetic  49.9 us (21%)
  waiting for transfers between devices  4.49 us (2%)
  loops' own time  4.19 us (2%)
    gather x32, local copies, waits for them, and re-layouts, tendency(): nearby = jnp.take(framed, centre + offsets[branch], axis=1)  58.2 us
    dot_general x2, matrix products, longwave(): jnp.dot(w_fraction.T, hidden, preferred_element_type=jnp.float32)  21.4 us
    ppermute x2, starting transfers between devices, extended(): lax.ppermute(head, axis, [((i + 1) % count, i) for i in range(count)])  18 us
    dot_general x2, matrix products, longwave(): jnp.dot(w_depth.T, hidden, preferred_element_type=jnp.float32)  17 us
    ppermute x3, starting transfers between devices, swapped(): lax.ppermute(value, axis, [(i, i ^ 1 << stride) for i in range(lax.axis_s...  16.2 us
    another operation x2, other arithmetic, longwave(): above = jnp.cumsum(depth, axis=1) - depth  14.5 us
    reduce_sum x1, other arithmetic, shortwave(): return heat_scale / depth.shape[0] * jnp.sum(beam, axis=0)  10.5 us
    dot_general x1, matrix products, shortwave(): jnp.dot(w_depth.T, hidden, preferred_element_type=jnp.float32)  8.19 us
  transfers between devices with their start and end apart: 10, of which 3 were waited for; matrix products, arithmetic and copies ran while one was open for 72% of the time, Pallas kernels for 0%

commit v1 on v0

v1 whole, which is shorter than its diff:
```python
import functools
import math

import jax
import jax.numpy as jnp
from jax import lax
from jax.experimental import pallas as pl
from jax.experimental.pallas import tpu as pltpu
from jax.sharding import PartitionSpec as P

COL_DEV = 256
HALF = 128
TILE = 1024
NB = 4
HW = 256
GAS = 7
f32, bf16 = jnp.float32, jnp.bfloat16
MESH = pl.DeviceIdType.MESH
LOG2E = 1.4426950408889634
CLAMP = 120.0

def silu(x):
    return 0.5 * x * (1.0 + jnp.tanh(0.5 * x))

def soft2(y):
    return jnp.maximum(y, jnp.log2(1.0 + jnp.exp2(jnp.minimum(y, CLAMP))))

def hi_lo(w):
    hi = w.astype(bf16)
    return hi, (w - hi.astype(f32)).astype(bf16)

def prep_first(w_first):
    wt = jnp.transpose(w_first.astype(f32))
    col = lax.broadcasted_iota(jnp.int32, (8, 128), 1)
    row = lax.broadcasted_iota(jnp.int32, (8, 128), 0)
    spread = (col // 16 == row).astype(f32)
    wide = jnp.dot(wt.astype(bf16), spread.astype(bf16), preferred_element_type=f32)
    return wide

def rad_kernel(cols_ref, work_ref, mu_ref, lw1_ref, lb_ref, lw2_ref, ld_ref, lf_ref, sw1_ref, sb_ref, sw2_ref, sd_ref, flux_ref,
               lw_out, sw_out, a1, b1, a2, b2, ah, bh, h1, h2, s_ref, e_ref, ss_ref, *, which):
    def first_into(dst, w_ref):
        wide = prep_first(w_ref[...])
        lane = lax.broadcasted_iota(jnp.int32, (64, 128), 1) % 16
        for l in range(16):
            dst[l * 64:(l + 1) * 64, :] = jnp.where(lane == l, wide, 0.0).astype(bf16)
    def second_into(dst, w_ref):
        wt = jnp.transpose(w_ref[...].astype(f32))
        z = jnp.zeros((64, 64), f32)
        for i in range(2):
            dst[i*64:(i+1)*64, :] = jnp.concatenate([wt if j == i else z for j in range(2)], axis=1).astype(bf16)
    first_into(a1, lw1_ref); first_into(b1, sw1_ref)
    second_into(a2, lw2_ref); second_into(b2, sw2_ref)
    d = jnp.transpose(ld_ref[...].astype(f32)) * LOG2E
    f = jnp.transpose(lf_ref[...].astype(f32)) * LOG2E
    inter = jnp.concatenate([d.reshape(32, 8, 64), f.reshape(32, 8, 64)], axis=1).reshape(512, 64)
    hi, lo = hi_lo(inter)
    ah[...] = jnp.concatenate([hi, lo], axis=1)
    sd = jnp.transpose(sd_ref[...].astype(f32)) * LOG2E
    hi, lo = hi_lo(sd)
    bh[...] = jnp.concatenate([hi, lo], axis=1)

    bl = jnp.transpose(jnp.broadcast_to(lb_ref[...], (128, 64)))
    bs = jnp.transpose(jnp.broadcast_to(sb_ref[...], (128, 64)))
    lbias = jnp.concatenate([bl, bl], axis=1)

    def hidden(x_ref, first, second, bias, width, blk):
        x = x_ref[:, pl.ds(pl.multiple_of(blk * 16, 16), 16), :].reshape(128, width)
        for q in range(8):
            pre = jnp.dot(first[q*128:(q+1)*128, :], x, preferred_element_type=f32)
            pre = pre.reshape(2, 64, width) + bias[None]
            one = silu(pre).reshape(128, width).astype(bf16)
            two = silu(jnp.dot(second[...], one, preferred_element_type=f32))
            h2[q*128:(q+1)*128, :width] = two.astype(bf16)

    if "l" in which:
        s_ref[...] = jnp.zeros_like(s_ref)
        e_ref[...] = jnp.ones_like(e_ref)
        @pl.loop(0, 4)
        def _(blk):
            hidden(cols_ref, a1, a2, lbias, 256, blk)
            @pl.loop(0, 16)
            def _(l):
                h = h2[pl.ds(pl.multiple_of(l * 64, 64), 64), :]
                hh = jnp.concatenate([h, h], axis=0)
                y = jnp.dot(ah[...], hh, preferred_element_type=f32)
                acc = jnp.zeros((8, 256), f32)
                for g in range(32):
                    tau = soft2(y[g*16:g*16+8])
                    frac = soft2(y[g*16+8:g*16+16])
                    s = s_ref[g*8:g*8+8] + tau
                    s_ref[g*8:g*8+8] = s
                    e = jnp.exp2(-0.1 * s)
                    acc = acc + frac * (e_ref[g*8:g*8+8] - e)
                    e_ref[g*8:g*8+8] = e
                lw_out[pl.ds(blk*16 + l, 1), :] = jnp.sum(acc, axis=0, keepdims=True)
        t = cols_ref[0].astype(f32)
        lw_out[...] = lw_out[...] * (-(12.0 / 256) * math.log(2.0)) * jnp.exp(0.25 * t)
    else:
        lw_out[...] = jnp.zeros_like(lw_out)
    if "s" in which:
        mu = mu_ref[...]
        slope = jnp.broadcast_to(-0.1 / mu, (8, 128))
        muf = jnp.broadcast_to(10.0 * mu, (224, 128))
        lf2 = jnp.transpose(jnp.broadcast_to(jnp.log2(flux_ref[...]), (128, 224)))
        ss_ref[...] = -muf * lf2
        g0 = jnp.sum(jnp.exp2(lf2), axis=0, keepdims=True)
        carry0 = g0
        def blk_body(blk, prev):
            hidden(work_ref, b1, b2, bs, 128, blk)
            def lev(lp, prev):
                r = pl.multiple_of(lp * 128, 128)
                h = jnp.concatenate([h2[pl.ds(r, 64), :128], h2[pl.ds(r + 64, 64), :128]], axis=1)
                hh = jnp.concatenate([h, h], axis=0)
                y = jnp.dot(bh[...], hh, preferred_element_type=f32)
                acc0 = jnp.zeros((8, 128), f32)
                acc1 = jnp.zeros((8, 128), f32)
                for g in range(28):
                    s = ss_ref[g*8:g*8+8]
                    s = s + soft2(y[g*8:g*8+8, :128])
                    acc0 = acc0 + jnp.exp2(s * slope)
                    s = s + soft2(y[g*8:g*8+8, 128:])
                    ss_ref[g*8:g*8+8] = s
                    acc1 = acc1 + jnp.exp2(s * slope)
                c0 = jnp.sum(acc0, axis=0, keepdims=True)
                c1 = jnp.sum(acc1, axis=0, keepdims=True)
                sw_out[pl.ds(blk*16 + lp*2, 1), :] = prev - c0
                sw_out[pl.ds(blk*16 + lp*2 + 1, 1), :] = c0 - c1
                return c1
            return lax.fori_loop(0, 8, lev, prev)
        lax.fori_loop(0, 4, blk_body, carry0)
        sw_out[...] = sw_out[...] * mu * (12.0 / 224)
    else:
        sw_out[...] = jnp.zeros_like(sw_out)

def radiate(cols, work, mu, lw, sw, which="ls"):
    lw1, lb, lw2, ld, lf = lw
    sw1, sb, sw2, sd, fl = sw
    return pl.pallas_call(
        functools.partial(rad_kernel, which=which),
        out_shape=(jax.ShapeDtypeStruct((64, 256), f32), jax.ShapeDtypeStruct((64, 128), f32)),
        in_specs=[pl.BlockSpec(memory_space=pltpu.VMEM)] * 13,
        out_specs=[pl.BlockSpec(memory_space=pltpu.VMEM)] * 2,
        scratch_shapes=[pltpu.VMEM((1024, 128), bf16), pltpu.VMEM((1024, 128), bf16), pltpu.VMEM((128, 128), bf16), pltpu.VMEM((128, 128), bf16),
                        pltpu.VMEM((512, 128), bf16), pltpu.VMEM((224, 128), bf16), pltpu.VMEM((1024, 256), bf16), pltpu.VMEM((1024, 256), bf16),
                        pltpu.VMEM((256, 256), f32), pltpu.VMEM((256, 256), f32), pltpu.VMEM((224, 128), f32)],
        compiler_params=pltpu.CompilerParams(vmem_limit_bytes=50 * 2**20), name="rad_" + which,
    )(cols, work, mu, lw1, lb.reshape(1, 64), lw2, ld, lf, sw1, sb.reshape(1, 64), sw2, sd, fl.reshape(1, 224))


N_GROUP = 4
WIDE = TILE + 6 * HW
TABLE = TILE + 4 * HW


def section(src, tables, weights, src_shift, lo, hi, put):
    @pl.loop(lo, hi)
    def _(b):
        at = lambda j: pl.ds(pl.multiple_of(j * 128, 128), 128)
        reach = [src[:, at(b - src_shift - 2 + s)] for s in range(5)]
        mid = reach[2]
        home = lax.rem(b + 2, 8) * 128
        total = jnp.zeros_like(mid)
        for k in range(NB):
            rel = jnp.broadcast_to(tables[k : k + 1, at(b - 2)] - home, mid.shape)
            lane = jnp.bitwise_and(rel, 127)
            which = jnp.right_shift(rel, 7)
            near = taken(reach[0], lane)
            for s in range(1, 5):
                near = jnp.where(which == s, taken(reach[s], lane), near)
            total = total + weights[k : k + 1, at(b - 2)] * (near - mid)
        put(b, at, mid, total)


def taken(rows, lane):
    parts = [
        jnp.take_along_axis(rows[i : i + 8], lane[i : i + 8], axis=1, mode="promise_in_bounds")
        for i in range(0, rows.shape[0], 8)
    ]
    return jnp.concatenate(parts, axis=0)


def greet(group_peers, tile_peers):
    barrier = pltpu.get_barrier_semaphore()
    for p in group_peers:
        pl.semaphore_signal(barrier, inc=1, device_id={"group": p}, device_id_type=MESH)
    for p in tile_peers:
        pl.semaphore_signal(barrier, inc=1, device_id={"tile": p}, device_id_type=MESH)
    pl.semaphore_wait(barrier, len(group_peers) + len(tile_peers))


def slots_of(listing):
    cols = lax.broadcasted_iota(jnp.int32, (COL_DEV, COL_DEV), 0)
    slot = lax.broadcasted_iota(jnp.int32, (COL_DEV, COL_DEV), 1).astype(f32)
    return jnp.sum(jnp.where(listing == cols, slot, 0.0), axis=1, keepdims=True)


def gather_kernel(
    pot, species, diff, nbr, listing_ref, count_ref, zen_ref,
    base_out, cols, work, mu_out,
    fe, f1, f2, te, third16, tables, weights, outgoing, arriving, mu_send, mu_arrive,
    local, h_send, h_recv, g_send, g_recv, t_send, t_recv, e_send, e_recv, d_send, d_recv,
):
    me, tile = lax.axis_index("group"), lax.axis_index("tile")
    n_tile = lax.axis_size("tile")
    right, left = lax.rem(tile + 1, n_tile), lax.rem(tile + n_tile - 1, n_tile)
    partner = tile + 1 - 2 * lax.rem(tile, 2)
    peers = [lax.rem(me + d, N_GROUP) for d in range(1, N_GROUP)]

    def remote(src, dst, send, recv, where):
        return pltpu.make_async_remote_copy(
            src_ref=src, dst_ref=dst, send_sem=send, recv_sem=recv,
            device_id=where, device_id_type=MESH)

    own = [
        pltpu.make_async_copy(pot, fe.at[:, 3 * HW : 3 * HW + TILE], local.at[0]),
        pltpu.make_async_copy(diff, weights.at[:, 2 * HW : 2 * HW + TILE], local.at[1]),
        pltpu.make_async_copy(nbr, tables.at[:, 2 * HW : 2 * HW + TILE], local.at[2]),
    ]
    levels = pl.ds(pl.multiple_of(me * 16, 16), 16)
    columns_of = lambda g: pl.ds(pl.multiple_of(g * COL_DEV, COL_DEV), COL_DEV)
    own_gas = pltpu.make_async_copy(
        species.at[:, :, columns_of(me)], cols.at[1 : GAS + 1, levels, :], local.at[3])
    for c in own:
        c.start()
    own_gas.start()
    greet(peers, (left, right))
    halo = [
        remote(pot.at[:, : 3 * HW], fe.at[:, 3 * HW + TILE :], h_send.at[0], h_recv.at[0], {"tile": left}),
        remote(pot.at[:, TILE - 3 * HW :], fe.at[:, : 3 * HW], h_send.at[1], h_recv.at[1], {"tile": right}),
        remote(diff.at[:, : 2 * HW], weights.at[:, 2 * HW + TILE :], h_send.at[2], h_recv.at[2], {"tile": left}),
        remote(diff.at[:, TILE - 2 * HW :], weights.at[:, : 2 * HW], h_send.at[3], h_recv.at[3], {"tile": right}),
        remote(nbr.at[:, : 2 * HW], tables.at[:, 2 * HW + TILE :], h_send.at[4], h_recv.at[4], {"tile": left}),
        remote(nbr.at[:, TILE - 2 * HW :], tables.at[:, : 2 * HW], h_send.at[5], h_recv.at[5], {"tile": right}),
    ]
    for c in halo:
        c.start()
    gas = [
        remote(species.at[:, :, columns_of(p)], cols.at[1 : GAS + 1, levels, :],
               g_send.at[i], g_recv.at[i], {"group": p})
        for i, p in enumerate(peers)
    ]
    for c in gas:
        c.start()
    for c in own:
        c.wait()
    for c in halo:
        c.wait()

    def put_first(b, at, mid, total):
        f1[:, at(b)] = mid + total

    def put_second(b, at, mid, total):
        f2[:, at(b)] = 0.75 * fe[:, at(b)] + 0.25 * (mid + total)

    def put_third(b, at, mid, total):
        value = fe[:, at(b)] / 3.0 + (2.0 / 3.0) * (mid + total)
        te[:, at(b - 4)] = value
        third16[:, at(b - 6)] = value.astype(bf16)

    section(fe, tables, weights, 0, 2, 18, put_first)
    section(f1, tables, weights, 0, 4, 16, put_second)
    section(f2, tables, weights, 0, 6, 14, put_third)

    warm = [
        remote(third16.at[:, columns_of(p)], cols.at[0, levels, :],
               t_send.at[i], t_recv.at[i], {"group": p})
        for i, p in enumerate(peers)
    ]
    for c in warm:
        c.start()
    edges = [
        remote(te.at[:, HW : 2 * HW], te.at[:, HW + TILE :], e_send.at[0], e_recv.at[0], {"tile": left}),
        remote(te.at[:, TILE : HW + TILE], te.at[:, :HW], e_send.at[1], e_recv.at[1], {"tile": right}),
    ]
    for c in edges:
        c.start()
    cols[0, levels, :] = third16[:, columns_of(me)]

    count = count_ref[...].astype(f32)
    slot = slots_of(listing_ref[...])
    place = lax.broadcasted_iota(jnp.int32, (COL_DEV, HALF), 1).astype(f32)
    kept = (slot == place) & (place < count)
    sent = (slot == place + count - HALF) & (place >= COL_DEV - count)
    pick = jnp.concatenate([kept.astype(f32), sent.astype(f32)], axis=1).astype(bf16)

    own_gas.wait()
    for c in gas:
        c.wait()
    for c in warm:
        c.wait()
    picked = jnp.dot(cols[...].reshape((GAS + 1) * 64, COL_DEV), pick, preferred_element_type=f32)
    outgoing[...] = picked[:, HALF:].astype(bf16).reshape(GAS + 1, 64, HALF)
    mu_picked = jnp.dot(jnp.broadcast_to(zen_ref[...], (16, COL_DEV)), pick, preferred_element_type=f32)
    mu_send[...] = mu_picked[:8, HALF:]
    swap = [
        remote(outgoing, arriving, d_send.at[0], d_recv.at[0], {"tile": partner}),
        remote(mu_send, mu_arrive, d_send.at[1], d_recv.at[1], {"tile": partner}),
    ]
    for c in swap:
        c.start()
    for c in edges:
        c.wait()

    def put_base(b, at, mid, total):
        base_out[:, at(b - 6)] = mid + total

    section(te, tables, weights, 4, 6, 14, put_base)
    for c in swap:
        c.wait()
    kept_cols = picked[:, :HALF].astype(bf16).reshape(GAS + 1, 64, HALF)
    work[...] = kept_cols + arriving[...]
    mu_out[...] = mu_picked[:1, :HALF] + mu_arrive[:1, :]


def spread_kernel(
    lw, sw, base, listing_ref, count_ref, out,
    ret, heat, slab, d_send, d_recv, s_send, s_recv,
):
    me, tile = lax.axis_index("group"), lax.axis_index("tile")
    partner = tile + 1 - 2 * lax.rem(tile, 2)
    peers = [lax.rem(me + d, N_GROUP) for d in range(1, N_GROUP)]

    def remote(src, dst, send, recv, where):
        return pltpu.make_async_remote_copy(
            src_ref=src, dst_ref=dst, send_sem=send, recv_sem=recv,
            device_id=where, device_id_type=MESH)

    greet(peers, (partner,))
    back = remote(sw, ret, d_send, d_recv, {"tile": partner})
    back.start()
    count = count_ref[...].astype(f32)
    slot = slots_of(listing_ref[...])
    diag = lax.broadcasted_iota(jnp.int32, (COL_DEV, COL_DEV), 0) == lax.broadcasted_iota(
        jnp.int32, (COL_DEV, COL_DEV), 1)
    slot = jnp.sum(jnp.where(diag, slot, 0.0), axis=0, keepdims=True)
    here = slot < jnp.minimum(count, HALF)
    there = (slot >= HALF) & (slot < count)
    index = jnp.where(there, slot + HALF - count, slot).astype(jnp.int32)
    index = jnp.bitwise_and(index, HALF - 1)
    here, there = here.astype(f32), there.astype(f32)
    back.wait()
    for half in range(2):
        part = slice(half * HALF, half * HALF + HALF)
        lane = jnp.broadcast_to(index[:, part], (64, HALF))
        heat[:, part] = (
            lw[:, part]
            + here[:, part] * taken(sw[...], lane)
            + there[:, part] * taken(ret[...], lane)
        )
    levels_of = lambda g: pl.ds(pl.multiple_of(g * 16, 16), 16)
    columns = pl.ds(pl.multiple_of(me * COL_DEV, COL_DEV), COL_DEV)
    sends = [
        remote(heat.at[levels_of(p), :], slab.at[:, columns], s_send.at[i], s_recv.at[i], {"group": p})
        for i, p in enumerate(peers)
    ]
    for c in sends:
        c.start()
    slab[:, columns] = heat[levels_of(me), :]
    for c in sends:
        c.wait()
    out[...] = base[...] + slab[...]


VMEM = pl.BlockSpec(memory_space=pltpu.VMEM)
ANY = pl.BlockSpec(memory_space=pl.ANY)


def per_device(
    potential, species_inputs, diffusion, neighbours, sunlit_column_index, day_count, zenith,
    lw_first, lw_bias, lw_second, lw_depth, lw_fraction,
    sw_first, sw_bias, sw_second, sw_depth, solar_flux,
):
    listing = sunlit_column_index.reshape(1, COL_DEV)
    dma = pltpu.SemaphoreType.DMA
    base, cols, work, mu = pl.pallas_call(
        gather_kernel,
        out_shape=(
            jax.ShapeDtypeStruct((16, TILE), f32),
            jax.ShapeDtypeStruct((8, 64, COL_DEV), bf16),
            jax.ShapeDtypeStruct((8, 64, HALF), bf16),
            jax.ShapeDtypeStruct((1, HALF), f32),
        ),
        in_specs=[ANY, ANY, ANY, ANY, VMEM, VMEM, VMEM],
        out_specs=[VMEM] * 4,
        scratch_shapes=[
            pltpu.VMEM((16, WIDE), f32),
            pltpu.VMEM((16, WIDE), f32),
            pltpu.VMEM((16, WIDE), f32),
            pltpu.VMEM((16, TILE + 2 * HW), f32),
            pltpu.VMEM((16, TILE), bf16),
            pltpu.VMEM((NB, TABLE), jnp.int32),
            pltpu.VMEM((NB, TABLE), f32),
            pltpu.VMEM((8, 64, HALF), bf16),
            pltpu.VMEM((8, 64, HALF), bf16),
            pltpu.VMEM((8, HALF), f32),
            pltpu.VMEM((8, HALF), f32),
            dma((4,)), dma((6,)), dma((6,)), dma((3,)), dma((3,)), dma((3,)), dma((3,)),
            dma((2,)), dma((2,)), dma((2,)), dma((2,)),
        ],
        compiler_params=pltpu.CompilerParams(
            collective_id=0, has_side_effects=True, vmem_limit_bytes=24 * 2**20),
        name="gather",
    )(potential, species_inputs, diffusion, neighbours, listing, day_count, zenith.reshape(1, COL_DEV))
    lw, sw = radiate(
        cols, work, mu,
        (lw_first, lw_bias, lw_second, lw_depth, lw_fraction),
        (sw_first, sw_bias, sw_second, sw_depth, solar_flux))
    return pl.pallas_call(
        spread_kernel,
        out_shape=jax.ShapeDtypeStruct((16, TILE), f32),
        in_specs=[VMEM] * 5,
        out_specs=VMEM,
        scratch_shapes=[
            pltpu.VMEM((64, HALF), f32),
            pltpu.VMEM((64, COL_DEV), f32),
            pltpu.VMEM((16, TILE), f32),
            dma(()), dma(()), dma((3,)), dma((3,)),
        ],
        compiler_params=pltpu.CompilerParams(
            collective_id=1, has_side_effects=True, vmem_limit_bytes=16 * 2**20),
        name="spread",
    )(lw, sw, base, listing, day_count)


def solution(mesh):
    return jax.shard_map(
        per_device,
        mesh=mesh,
        in_specs=(
            P("group", "tile"), P(None, "group", "tile"), P(None, "tile"), P(None, "tile"),
            P("group", "tile", None), P("group", "tile"), P("group", "tile", None),
            P(), P(), P(), P(), P(), P(), P(), P(), P(), P(),
        ),
        out_specs=P("group", "tile"),
        check_vma=False,
    )
```

time: 238 us -> 88.2 us (0.37)
  Pallas kernels: 0 us -> 81.8 us
  local copies, waits for them, and re-layouts: 69.7 us -> 5.17 us
  matrix products: 55.9 us -> 0 us
  starting transfers between devices: 51 us -> 0 us
  other arithmetic: 49.9 us -> 0 us
  waiting for transfers between devices: 4.49 us -> 0 us
  loops' own time: 4.19 us -> 0 us
    pallas_call x0 -> x3, Pallas kernels: none -> 81.8 us  [the longest x1 36.4 us: radiate(): pl.pallas_call(functools.partial(rad_kernel, which=which), out_shape=(jax...]
    gather x32 -> x0, local copies, waits for them, and re-layouts: 58.2 us -> none  [tendency(): nearby = jnp.take(framed, centre + offsets[branch], axis=1)]
    dot_general x17 -> x0, matrix products: 55.9 us -> none  [the longest x2 21.4 us: longwave(): jnp.dot(w_fraction.T, hidden, preferred_element_type=jnp.float32)]
    ppermute x7 -> x0, starting transfers between devices: 39.8 us -> none  [the longest x2 18 us: extended(): lax.ppermute(head, axis, [((i + 1) % count, i) for i in range(count)])]
    another operation x3 -> x0, other arithmetic: 21 us -> none  [the longest x2 14.5 us: longwave(): above = jnp.cumsum(depth, axis=1) - depth]
    all_to_all x3 -> x0, starting transfers between devices: 11.2 us -> none  [the longest x2 6.65 us: several_exchanges(): lax.all_to_all(slab, axis, split_axis=0, concat_axis=0, tiled=True)]
    reduce_sum x1 -> x0, other arithmetic: 10.5 us -> none  [shortwave(): return heat_scale / depth.shape[0] * jnp.sum(beam, axis=0)]
    gather x16 -> x0, other arithmetic: 5.54 us -> none
  transfers between devices with their start and end apart: 10 -> 0, of which waited for: 3 -> 0; matrix products, arithmetic and copies ran while one was open for 72% -> 0% of each run, Pallas kernels for 0% -> 0%
where the time goes in v1:
time: 88.2 us; the launch traced here: 87.7 us
  Pallas kernels  81.8 us (93%)
  local copies, waits for them, and re-layouts  5.17 us (6%)
    pallas_call x1, Pallas kernels, radiate(): pl.pallas_call(functools.partial(rad_kernel, which=which), out_shape=(jax...  36.4 us
    pallas_call x1, Pallas kernels, per_device(): pl.pallas_call(gather_kernel, out_shape=(jax.ShapeDtypeStruct((16, TILE),...  33 us
    pallas_call x1, Pallas kernels, per_device(): pl.pallas_call(spread_kernel, out_shape=jax.ShapeDtypeStruct((16, TILE),...  12.4 us
    unnamed x33, local copies, waits for them, and re-layouts  5.17 us

profile of v1, /device:TPU:1, one launch (start us, length us, event | category | flops | bytes accessed | tf_op | source)
XLA Modules:
  0.0 87.7 jit_solution(9854409093364060013)
XLA Ops:
  0.7 0.0 copy-start.12
  0.7 0.0 copy-start.9
  0.7 0.7 copy-done.12
  1.3 0.0 copy-done.9
  1.3 0.0 copy-start
  1.4 0.9 %copy-done = bf16[7,16,1024]{2,1,0:T(8,128)(2,1)S(1)} copy-done((bf16[7,16,1024]{2,1,0:T(8,128)(2,1)S(1)}, bf16[7,16,1024]{2,1,0:T(8,128)(2,1)}, u32[]{:S(2)}) %copy-start) | copy-done | bytes 229400
  2.3 0.0 copy-start.1
  2.3 0.8 copy-done.1
  3.1 0.0 copy-start.5
  3.1 0.7 copy-done.5
  3.8 0.0 copy-start.6
  3.8 0.7 copy-done.6
  4.6 0.0 copy-start.2
  4.6 0.0 copy-start.3
  4.6 0.0 copy-start.4
  4.6 0.0 copy-start.7
  4.6 0.0 copy-start.8
  4.6 0.0 copy-start.15
  4.6 33.0 %gather.1 = (f32[16,1024]{1,0:T(8,128)S(1)}, bf16[8,64,256]{2,1,0:T(8,128)(2,1)S(1)}, bf16[8,64,128]{2,1,0:T(8,128)(2,1)S(1)}, f32[1,128]{1,0:T(1,128)S(1)}) custom-call(f32[16,1024]{1,0:T(8,128)S(1)} %copy-done.1, bf16[7,16,1024]{2,1,0:T(8,128)(2,1)S(1)} %copy-done, f32[4,1024]{1,0:T(4,128)S(1)} %copy-done.5, s32[4,1024]{1,0:T(4,128)S(1)} %copy-done.6, ...), custom_call_target="tpu_custom_call" | custom-call | tf_op jit(solution)/shard_map/gather/pallas_call | solution.py:376
  37.6 0.0 copy-start.11
  37.6 0.0 copy-start.10
  37.6 0.0 copy-start.13
  37.6 0.0 copy-start.14
  37.6 0.0 copy-done.2
  37.6 0.0 copy-done.3
  37.7 0.0 copy-done.4
  37.7 0.0 copy-done.7
  37.7 0.0 copy-done.8
  37.7 0.0 copy-done.15
  37.7 0.6 copy-done.11
  38.3 0.0 copy-done.10
  38.3 0.0 copy-done.13
  38.3 0.0 copy-done.14
  38.3 36.4 %rad_ls.1 = (f32[64,256]{1,0:T(8,128)S(1)}, f32[64,128]{1,0:T(8,128)S(1)}) custom-call(bf16[8,64,256]{2,1,0:T(8,128)(2,1)S(1)} %get-tuple-element.11.cols_ref, bf16[8,64,128]{2,1,0:T(8,128)(2,1)S(1)} %get-tuple-element.12.work_ref, f32[1,128]{1,0:T(1,128)S(1)} %get-tuple-element.13.mu_ref, bf16[8,64]{1,0:T(8,128)(2,1)S(1)} %copy-done.10, ...), custom_call_target="tpu_custom_call" | custom-call | tf_op jit(solution)/shard_map/rad_ls/pallas_call | solution.py:139
  74.7 12.4 %spread.1 = f32[16,1024]{1,0:T(8,128)S(1)} custom-call(f32[64,256]{1,0:T(8,128)S(1)} %get-tuple-element.14.lw, f32[64,128]{1,0:T(8,128)S(1)} %get-tuple-element.15.sw, f32[16,1024]{1,0:T(8,128)S(1)} %get-tuple-element.16.base, s32[1,256]{1,0:T(1,128)S(1)} %bitcast.6, s32[1,1]{1,0:T(1,128)S(6)} %copy.19.count_ref), custom_call_target="tpu_custom_call" | custom-call | tf_op jit(solution)/shard_map/spread/pallas_call | solution.py:409
  87.1 0.6 copy.20
Async XLA Ops:
  0.7 0.7 copy-start.12
  0.7 0.7 copy-start.9
  1.3 0.9 %copy-start = (bf16[7,16,1024]{2,1,0:T(8,128)(2,1)S(1)}, bf16[7,16,1024]{2,1,0:T(8,128)(2,1)}, u32[]{:S(2)}) copy-start(bf16[7,16,1024]{2,1,0:T(8,128)(2,1)} %species.1) | copy-start | bytes 688132
  2.3 0.8 copy-start.1
  3.1 0.7 copy-start.5
  3.8 0.7 copy-start.6
  4.6 33.1 %copy-start.2 = (bf16[64,256]{1,0:T(8,128)(2,1)S(1)}, bf16[64,256]{1,0:T(8,128)(2,1)}, u32[]{:S(2)}) copy-start(bf16[64,256]{1,0:T(8,128)(2,1)} %ld_ref.1) | copy-start | bytes 98308
  4.6 33.1 %copy-start.3 = (bf16[64,256]{1,0:T(8,128)(2,1)S(1)}, bf16[64,256]{1,0:T(8,128)(2,1)}, u32[]{:S(2)}) copy-start(bf16[64,256]{1,0:T(8,128)(2,1)} %lf_ref.1) | copy-start | bytes 98308
  4.6 33.1 %copy-start.4 = (bf16[64,224]{1,0:T(8,128)(2,1)S(1)}, bf16[64,224]{1,0:T(8,128)(2,1)}, u32[]{:S(2)}) copy-start(bf16[64,224]{1,0:T(8,128)(2,1)} %sd_ref.1) | copy-start | bytes 86020
  4.6 33.1 %copy-start.7 = (bf16[64,64]{1,0:T(8,128)(2,1)S(1)}, bf16[64,64]{1,0:T(8,128)(2,1)}, u32[]{:S(2)}) copy-start(bf16[64,64]{1,0:T(8,128)(2,1)} %lw2_ref.1) | copy-start | bytes 24580
  4.6 33.1 %copy-start.8 = (bf16[64,64]{1,0:T(8,128)(2,1)S(1)}, bf16[64,64]{1,0:T(8,128)(2,1)}, u32[]{:S(2)}) copy-start(bf16[64,64]{1,0:T(8,128)(2,1)} %sw2_ref.1) | copy-start | bytes 24580
  4.6 33.1 %copy-start.15 = (f32[64]{0:T(128)S(1)}, f32[64]{0:T(128)}, u32[]{:S(2)}) copy-start(f32[64]{0:T(128)} %param.30) | copy-start | bytes 772
  37.6 0.7 copy-start.11
  37.6 0.7 copy-start.10
  37.6 0.7 copy-start.13
  37.6 0.7 copy-start.14

commit v2 on v1

v2 whole, which is shorter than its diff:
```python
import math

import jax
import jax.numpy as jnp
from jax import lax
from jax.experimental import pallas as pl
from jax.experimental.pallas import tpu as pltpu
from jax.sharding import PartitionSpec as P

COL_DEV = 256
HALF = 128
TILE = 1024
NB = 4
HW = 256
GAS = 7
f32, bf16 = jnp.float32, jnp.bfloat16
MESH = pl.DeviceIdType.MESH

LOG2E = 1.4426950408889634
CLAMP = 120.0
N_GROUP = 4
WIDE = TILE + 6 * HW
TABLE = TILE + 4 * HW
LEV = 64
PAIR = 2


def silu(x):
    half = 0.5 * x
    return half + half * jnp.tanh(half)


def soft2(y):
    return jnp.maximum(y, jnp.log2(1.0 + jnp.exp2(jnp.minimum(y, CLAMP))))


def in_two(w):
    high = w.astype(bf16)
    return jnp.concatenate([high, (w - high.astype(f32)).astype(bf16)], axis=1)


def turned(w):
    return jnp.transpose(w.astype(f32))


def spread_first(dst, w_ref):
    col = lax.broadcasted_iota(jnp.int32, (8, 128), 1)
    row = lax.broadcasted_iota(jnp.int32, (8, 128), 0)
    spread = (col // 16 == row).astype(f32).astype(bf16)
    wide = jnp.dot(turned(w_ref[...]).astype(bf16), spread, preferred_element_type=f32)
    lane = jnp.bitwise_and(lax.broadcasted_iota(jnp.int32, (64, 128), 1), 15)
    for l in range(16):
        dst[l * 64 : (l + 1) * 64, :] = jnp.where(lane == l, wide, 0.0).astype(bf16)


def two_blocks(dst, w_ref):
    wt = turned(w_ref[...])
    zero = jnp.zeros((64, 64), f32)
    dst[:64, :] = jnp.concatenate([wt, zero], axis=1).astype(bf16)
    dst[64:, :] = jnp.concatenate([zero, wt], axis=1).astype(bf16)


def down(row, width):
    return jnp.transpose(jnp.broadcast_to(row, (128, width)))


def hidden(h2, x_ref, first, second, bias, width, blk):
    x = x_ref[:, pl.ds(pl.multiple_of(blk * 16, 16), 16), :].reshape(128, width)
    for q in range(8):
        pre = jnp.dot(first[q * 128 : (q + 1) * 128, :], x, preferred_element_type=f32)
        one = silu(pre.reshape(2, 64, width) + bias[None]).reshape(128, width).astype(bf16)
        two = silu(jnp.dot(second[...], one, preferred_element_type=f32))
        h2[q * 128 : (q + 1) * 128, :width] = two.astype(bf16)


def longwave(lo, hi, cols, h2, a1, a2, bias, heads, s_ref, e_ref, lw):
    @pl.loop(lo, hi)
    def _(blk):
        hidden(h2, cols, a1, a2, bias[...], COL_DEV, blk)
        for i in range(16 // PAIR):
            h = jnp.concatenate(
                [h2[(i * PAIR + u) * 64 : (i * PAIR + u + 1) * 64, :] for u in range(PAIR)], axis=1)
            y = jnp.dot(heads[...], jnp.concatenate([h, h], axis=0), preferred_element_type=f32)
            totals = [jnp.zeros((8, COL_DEV), f32) for _ in range(PAIR)]
            for g in range(32):
                rows = slice(g * 8, g * 8 + 8)
                s = s_ref[rows]
                above = e_ref[rows]
                for u in range(PAIR):
                    at = slice(u * COL_DEV, (u + 1) * COL_DEV)
                    s = s + soft2(y[g * 16 : g * 16 + 8, at])
                    frac = soft2(y[g * 16 + 8 : g * 16 + 16, at])
                    below = jnp.exp2(-0.1 * s)
                    totals[u] = totals[u] + frac * (above - below)
                    above = below
                s_ref[rows] = s
                e_ref[rows] = above
            for u in range(PAIR):
                lw[pl.ds(blk * 16 + i * PAIR + u, 1), :] = jnp.sum(totals[u], axis=0, keepdims=True)


def shortwave(work, h2, b1, b2, bias, heads, log_flux, mu, ss_ref, sw):
    slope = jnp.broadcast_to(-0.1 / mu, (8, HALF))
    ss_ref[...] = jnp.broadcast_to(-10.0 * mu, (224, HALF)) * log_flux[...]
    top = jnp.sum(jnp.exp2(log_flux[...]), axis=0, keepdims=True)

    def block(blk, above):
        hidden(h2, work, b1, b2, bias[:, :HALF], HALF, blk)
        for i in range(8):
            r = i * 128
            h = jnp.concatenate([h2[r : r + 64, :HALF], h2[r + 64 : r + 128, :HALF]], axis=1)
            y = jnp.dot(heads[...], jnp.concatenate([h, h], axis=0), preferred_element_type=f32)
            upper = jnp.zeros((8, HALF), f32)
            lower = jnp.zeros((8, HALF), f32)
            for g in range(28):
                rows = slice(g * 8, g * 8 + 8)
                s = ss_ref[rows] + soft2(y[rows, :HALF])
                upper = upper + jnp.exp2(s * slope)
                s = s + soft2(y[rows, HALF:])
                ss_ref[rows] = s
                lower = lower + jnp.exp2(s * slope)
            upper = jnp.sum(upper, axis=0, keepdims=True)
            lower = jnp.sum(lower, axis=0, keepdims=True)
            sw[pl.ds(blk * 16 + i * 2, 1), :] = above - upper
            sw[pl.ds(blk * 16 + i * 2 + 1, 1), :] = upper - lower
            above = lower
        return above

    lax.fori_loop(0, 4, block, top)
    sw[...] = sw[...] * (mu * (12.0 / 224))


def section(src, tables, weights, src_shift, lo, hi, put):
    def step(b, c):
        at = lambda j: pl.ds(pl.multiple_of(j * 128, 128), 128)
        reach = [src[:, at(b - src_shift - 2 + s)] for s in range(5)]
        mid = reach[2]
        home = lax.rem(b + 2, 8) * 128
        total = jnp.zeros_like(mid)
        for k in range(NB):
            rel = jnp.broadcast_to(tables[k : k + 1, at(b - 2)] - home, (8, 128))
            lane = jnp.bitwise_and(rel, 127)
            which = jnp.right_shift(rel, 7)
            near = []
            for h in (0, 8):
                part = taken(reach[0][h : h + 8], lane)
                for s in range(1, 5):
                    part = jnp.where(which == s, taken(reach[s][h : h + 8], lane), part)
                near.append(part)
            near = jnp.concatenate(near, axis=0)
            total = total + weights[k : k + 1, at(b - 2)] * (near - mid)
        put(b, at, mid, total)
        return c

    lax.fori_loop(lo, hi, step, 0, unroll=4)


def taken(rows, lane):
    return jnp.take_along_axis(rows, lane, axis=1, mode="promise_in_bounds")


def slots_of(listing):
    cols = lax.broadcasted_iota(jnp.int32, (COL_DEV, COL_DEV), 0)
    slot = lax.broadcasted_iota(jnp.int32, (COL_DEV, COL_DEV), 1).astype(f32)
    return jnp.sum(jnp.where(listing == cols, slot, 0.0), axis=1, keepdims=True)


def kernel(
    pot, species, diff, nbr, lw1_h, lw2_h, ld_h, lf_h, sw1_h, sw2_h, sd_h,
    listing_ref, count_ref, zen_ref, lb_ref, sb_ref, flux_ref,
    out,
    fe, f1, f2, te, third16, base, tables, weights,
    cols, outgoing, arriving, work, mu_send, mu_arrive,
    lw1, lw2, ld, lf, sw1, sw2, sd,
    a1, a2, b1, b2, heads, sw_heads, lw_bias, sw_bias, log_flux, h2, s_ref, e_ref, ss_ref,
    lw, sw, ret, heat, slab,
    local, w_sem, h_send, h_recv, g_send, g_recv, t_send, t_recv, e_send, e_recv,
    d_send, d_recv, r_send, r_recv, s_send, s_recv,
):
    me, tile = lax.axis_index("group"), lax.axis_index("tile")
    n_tile = lax.axis_size("tile")
    right, left = lax.rem(tile + 1, n_tile), lax.rem(tile + n_tile - 1, n_tile)
    partner = tile + 1 - 2 * lax.rem(tile, 2)
    peers = [lax.rem(me + d, N_GROUP) for d in range(1, N_GROUP)]
    levels_of = lambda g: pl.ds(pl.multiple_of(g * 16, 16), 16)
    columns_of = lambda g: pl.ds(pl.multiple_of(g * COL_DEV, COL_DEV), COL_DEV)
    levels, columns = levels_of(me), columns_of(me)

    def remote(src, dst, send, recv, where):
        return pltpu.make_async_remote_copy(
            src_ref=src, dst_ref=dst, send_sem=send, recv_sem=recv,
            device_id=where, device_id_type=MESH)

    barrier = pltpu.get_barrier_semaphore()
    for p in (left, right):
        pl.semaphore_signal(barrier, inc=1, device_id={"tile": p}, device_id_type=MESH)
    for p in peers:
        pl.semaphore_signal(barrier, inc=1, device_id={"group": p}, device_id_type=MESH)

    own = [
        pltpu.make_async_copy(pot, fe.at[:, 3 * HW : 3 * HW + TILE], local.at[0]),
        pltpu.make_async_copy(diff, weights.at[:, 2 * HW : 2 * HW + TILE], local.at[1]),
        pltpu.make_async_copy(nbr, tables.at[:, 2 * HW : 2 * HW + TILE], local.at[2]),
        pltpu.make_async_copy(
            species.at[:, :, columns], cols.at[1 : GAS + 1, levels, :], local.at[3]),
    ]
    stage = [
        pltpu.make_async_copy(src, dst, w_sem.at[i])
        for i, (src, dst) in enumerate(
            [(lw1_h, lw1), (lw2_h, lw2), (ld_h, ld), (lf_h, lf), (sw1_h, sw1), (sw2_h, sw2), (sd_h, sd)])
    ]
    for c in own + stage:
        c.start()
    pl.semaphore_wait(barrier, N_GROUP + 1)

    halo = [
        remote(pot.at[:, : 3 * HW], fe.at[:, 3 * HW + TILE :], h_send.at[0], h_recv.at[0], {"tile": left}),
        remote(pot.at[:, TILE - 3 * HW :], fe.at[:, : 3 * HW], h_send.at[1], h_recv.at[1], {"tile": right}),
        remote(diff.at[:, : 2 * HW], weights.at[:, 2 * HW + TILE :], h_send.at[2], h_recv.at[2], {"tile": left}),
        remote(diff.at[:, TILE - 2 * HW :], weights.at[:, : 2 * HW], h_send.at[3], h_recv.at[3], {"tile": right}),
        remote(nbr.at[:, : 2 * HW], tables.at[:, 2 * HW + TILE :], h_send.at[4], h_recv.at[4], {"tile": left}),
        remote(nbr.at[:, TILE - 2 * HW :], tables.at[:, : 2 * HW], h_send.at[5], h_recv.at[5], {"tile": right}),
    ]
    gas = [
        remote(species.at[:, :, columns_of(p)], cols.at[1 : GAS + 1, levels, :],
               g_send.at[i], g_recv.at[i], {"group": p})
        for i, p in enumerate(peers)
    ]
    for c in halo + gas:
        c.start()

    for c in stage:
        c.wait()
    spread_first(a1, lw1)
    spread_first(b1, sw1)
    two_blocks(a2, lw2)
    two_blocks(b2, sw2)
    depth, frac = turned(ld[...]) * LOG2E, turned(lf[...]) * LOG2E
    woven = jnp.concatenate([depth.reshape(32, 8, 64), frac.reshape(32, 8, 64)], axis=1)
    heads[...] = in_two(woven.reshape(512, 64))
    sw_heads[...] = in_two(turned(sd[...]) * LOG2E)
    bias = down(lb_ref[...], 64)
    lw_bias[...] = jnp.concatenate([bias, bias], axis=1)
    sw_bias[...] = down(sb_ref[...], 64)
    log_flux[...] = down(jnp.log2(flux_ref[...]), 224)
    s_ref[...] = jnp.zeros_like(s_ref)
    e_ref[...] = jnp.ones_like(e_ref)
    count = count_ref[...].astype(f32)
    slot = slots_of(listing_ref[...])
    place = lax.broadcasted_iota(jnp.int32, (COL_DEV, HALF), 1).astype(f32)
    kept = (slot == place) & (place < count)
    sent = (slot == place + count - HALF) & (place >= COL_DEV - count)
    pick = jnp.concatenate([kept.astype(f32), sent.astype(f32)], axis=1).astype(bf16)
    mu_picked = jnp.dot(
        jnp.broadcast_to(zen_ref[...], (16, COL_DEV)), pick, preferred_element_type=f32)
    mu_send[...] = mu_picked[:8, HALF:]

    for c in own[:3]:
        c.wait()
    for c in halo:
        c.wait()

    def put_first(b, at, mid, total):
        f1[:, at(b)] = mid + total

    def put_second(b, at, mid, total):
        f2[:, at(b)] = 0.75 * fe[:, at(b)] + 0.25 * (mid + total)

    def put_third(b, at, mid, total):
        value = fe[:, at(b)] / 3.0 + (2.0 / 3.0) * (mid + total)
        te[:, at(b - 4)] = value
        third16[:, at(b - 6)] = value.astype(bf16)

    def put_base(b, at, mid, total):
        base[:, at(b - 6)] = mid + total

    section(fe, tables, weights, 0, 2, 18, put_first)
    section(f1, tables, weights, 0, 4, 16, put_second)
    section(f2, tables, weights, 0, 6, 14, put_third)

    warm = [
        remote(third16.at[:, columns_of(p)], cols.at[0, levels, :],
               t_send.at[i], t_recv.at[i], {"group": p})
        for i, p in enumerate(peers)
    ]
    edges = [
        remote(te.at[:, HW : 2 * HW], te.at[:, HW + TILE :], e_send.at[0], e_recv.at[0], {"tile": left}),
        remote(te.at[:, TILE : HW + TILE], te.at[:, :HW], e_send.at[1], e_recv.at[1], {"tile": right}),
    ]
    for c in warm + edges:
        c.start()
    cols[0, levels, :] = third16[:, columns]
    own[3].wait()
    for c in gas + warm:
        c.wait()

    picked = jnp.dot(
        cols[...].reshape((GAS + 1) * LEV, COL_DEV), pick, preferred_element_type=f32)
    outgoing[...] = picked[:, HALF:].astype(bf16).reshape(GAS + 1, LEV, HALF)
    swap = [
        remote(outgoing, arriving, d_send.at[0], d_recv.at[0], {"tile": partner}),
        remote(mu_send, mu_arrive, d_send.at[1], d_recv.at[1], {"tile": partner}),
    ]
    for c in swap:
        c.start()
    work[...] = picked[:, :HALF].astype(bf16).reshape(GAS + 1, LEV, HALF)

    longwave(0, 2, cols, h2, a1, a2, lw_bias, heads, s_ref, e_ref, lw)
    for c in swap:
        c.wait()
    work[...] = work[...] + arriving[...]
    mu = mu_picked[:1, :HALF] + mu_arrive[:1, :]
    shortwave(work, h2, b1, b2, sw_bias, sw_heads, log_flux, mu, ss_ref, sw)
    back = remote(sw, ret, r_send, r_recv, {"tile": partner})
    back.start()
    longwave(2, 4, cols, h2, a1, a2, lw_bias, heads, s_ref, e_ref, lw)

    diag = lax.broadcasted_iota(jnp.int32, (COL_DEV, COL_DEV), 0) == lax.broadcasted_iota(
        jnp.int32, (COL_DEV, COL_DEV), 1)
    slot = jnp.sum(jnp.where(diag, slot, 0.0), axis=0, keepdims=True)
    here = slot < jnp.minimum(count, HALF)
    there = (slot >= HALF) & (slot < count)
    index = jnp.where(there, slot + HALF - count, slot).astype(jnp.int32)
    index = jnp.bitwise_and(index, HALF - 1)
    here, there = here.astype(f32), there.astype(f32)
    back.wait()
    planck = jnp.exp(0.25 * cols[0].astype(f32)) * (-(12.0 / 256) * math.log(2.0))
    for half in range(2):
        part = slice(half * HALF, half * HALF + HALF)
        lane = jnp.broadcast_to(index[:, part], (8, HALF))
        for r in range(0, LEV, 8):
            rows = slice(r, r + 8)
            heat[rows, part] = (
                lw[rows, part] * planck[rows, part]
                + here[:, part] * taken(sw[rows, :], lane)
                + there[:, part] * taken(ret[rows, :], lane)
            )
    sends = [
        remote(heat.at[levels_of(p), :], slab.at[:, columns], s_send.at[i], s_recv.at[i], {"group": p})
        for i, p in enumerate(peers)
    ]
    for c in sends:
        c.start()
    slab[:, columns] = heat[levels, :]
    for c in edges:
        c.wait()
    section(te, tables, weights, 4, 6, 14, put_base)
    for c in sends:
        c.wait()
    out[...] = base[...] + slab[...]


VMEM = pl.BlockSpec(memory_space=pltpu.VMEM)
ANY = pl.BlockSpec(memory_space=pl.ANY)


def per_device(
    potential, species_inputs, diffusion, neighbours, sunlit_column_index, day_count, zenith,
    lw_first, lw_bias, lw_second, lw_depth, lw_fraction,
    sw_first, sw_bias, sw_second, sw_depth, solar_flux,
):
    dma = pltpu.SemaphoreType.DMA
    at32 = lambda *shape: pltpu.VMEM(shape, f32)
    at16 = lambda *shape: pltpu.VMEM(shape, bf16)
    return pl.pallas_call(
        kernel,
        out_shape=jax.ShapeDtypeStruct((16, TILE), f32),
        in_specs=[ANY] * 11 + [VMEM] * 6,
        out_specs=VMEM,
        scratch_shapes=[
            at32(16, WIDE), at32(16, WIDE), at32(16, WIDE), at32(16, TILE + 2 * HW),
            at16(16, TILE), at32(16, TILE),
            pltpu.VMEM((NB, TABLE), jnp.int32), at32(NB, TABLE),
            at16(8, LEV, COL_DEV), at16(8, LEV, HALF), at16(8, LEV, HALF), at16(8, LEV, HALF),
            at32(8, HALF), at32(8, HALF),
            at16(8, 64), at16(64, 64), at16(64, 256), at16(64, 256),
            at16(8, 64), at16(64, 64), at16(64, 224),
            at16(1024, 128), at16(128, 128), at16(1024, 128), at16(128, 128),
            at16(512, 128), at16(224, 128),
            at32(64, COL_DEV), at32(64, HALF), at32(224, HALF),
            at16(1024, COL_DEV), at32(256, COL_DEV), at32(256, COL_DEV), at32(224, HALF),
            at32(LEV, COL_DEV), at32(LEV, HALF), at32(LEV, HALF), at32(LEV, COL_DEV), at32(16, TILE),
            dma((4,)), dma((7,)), dma((6,)), dma((6,)), dma((3,)), dma((3,)), dma((3,)), dma((3,)),
            dma((2,)), dma((2,)), dma((2,)), dma((2,)), dma(()), dma(()), dma((3,)), dma((3,)),
        ],
        compiler_params=pltpu.CompilerParams(
            collective_id=0, has_side_effects=True, vmem_limit_bytes=60 * 2**20),
        name="step",
    )(
        potential, species_inputs, diffusion, neighbours,
        lw_first, lw_second, lw_depth, lw_fraction, sw_first, sw_second, sw_depth,
        sunlit_column_index.reshape(1, COL_DEV), day_count, zenith.reshape(1, COL_DEV),
        lw_bias.reshape(1, 64), sw_bias.reshape(1, 64), solar_flux.reshape(1, 224),
    )


def solution(mesh):
    return jax.shard_map(
        per_device,
        mesh=mesh,
        in_specs=(
            P("group", "tile"), P(None, "group", "tile"), P(None, "tile"), P(None, "tile"),
            P("group", "tile", None), P("group", "tile"), P("group", "tile", None),
            P(), P(), P(), P(), P(), P(), P(), P(), P(), P(),
        ),
        out_specs=P("group", "tile"),
        check_vma=False,
    )
```

time: 88.2 us -> 52.5 us (0.60)
  the two profiles are of different devices: /device:TPU:1 before, /device:TPU:32 now
where the time goes in v2:
time: 52.5 us; the launch traced here: 52.3 us
  Pallas kernels  50.2 us (96%)
  local copies, waits for them, and re-layouts  1.47 us (3%)
  between operations  0.66 us (1%)
    pallas_call x1, Pallas kernels, per_device(): pl.pallas_call(kernel, out_shape=jax.ShapeDtypeStruct((16, TILE), f32), i...  50.2 us
    unnamed x1, local copies, waits for them, and re-layouts  1.47 us

profile of v2, /device:TPU:32, one launch (start us, length us, event | category | flops | bytes accessed | tf_op | source)
XLA Modules:
  0.0 52.3 jit_solution(207303296770268745)
XLA Ops:
  0.7 50.2 %step.1 = f32[16,1024]{1,0:T(8,128)} custom-call(f32[16,1024]{1,0:T(8,128)} %pot.1, bf16[7,16,1024]{2,1,0:T(8,128)(2,1)} %species.1, f32[4,1024]{1,0:T(4,128)} %diff.1, s32[4,1024]{1,0:T(4,128)} %nbr.1, bf16[8,64]{1,0:T(8,128)(2,1)} %lw1_h.1, bf16[64,64]{1,0:T(8,128)(2,1)} %lw2_h.1, bf16[64,256]{1,0:T(8,128)(2,1)} %ld_h.1, bf16[64,256]{1,0:T(8,128)(2,1)} %lf_h.1, ...), custom_call_target="tpu_custom_call" | custom-call | tf_op jit(solution)/shard_map/step/pallas_call | solution.py:365
  50.9 1.5 %copy.20 = f32[16,1024]{1,0:T(8,128)} copy(f32[16,1024]{1,0:T(8,128)} %step.1) | data formatting | bytes 131072

commit v3 on v2

--- a/solution.py
+++ b/solution.py
@@ -100,30 +100,28 @@
 
 
 def shortwave(work, h2, b1, b2, bias, heads, log_flux, mu, ss_ref, sw):
-    slope = jnp.broadcast_to(-0.1 / mu, (8, HALF))
-    ss_ref[...] = jnp.broadcast_to(-10.0 * mu, (224, HALF)) * log_flux[...]
+    slope = jnp.broadcast_to(-0.1 / mu, (8, COL_DEV))
+    ss_ref[...] = jnp.broadcast_to(-10.0 * mu, (224, COL_DEV)) * log_flux[...]
     top = jnp.sum(jnp.exp2(log_flux[...]), axis=0, keepdims=True)
 
     def block(blk, above):
-        hidden(h2, work, b1, b2, bias[:, :HALF], HALF, blk)
-        for i in range(8):
-            r = i * 128
-            h = jnp.concatenate([h2[r : r + 64, :HALF], h2[r + 64 : r + 128, :HALF]], axis=1)
+        hidden(h2, work, b1, b2, bias[...], COL_DEV, blk)
+        for i in range(16 // PAIR):
+            h = jnp.concatenate(
+                [h2[(i * PAIR + u) * 64 : (i * PAIR + u + 1) * 64, :] for u in range(PAIR)], axis=1)
             y = jnp.dot(heads[...], jnp.concatenate([h, h], axis=0), preferred_element_type=f32)
-            upper = jnp.zeros((8, HALF), f32)
-            lower = jnp.zeros((8, HALF), f32)
+            totals = [jnp.zeros((8, COL_DEV), f32) for _ in range(PAIR)]
             for g in range(28):
                 rows = slice(g * 8, g * 8 + 8)
-                s = ss_ref[rows] + soft2(y[rows, :HALF])
-                upper = upper + jnp.exp2(s * slope)
-                s = s + soft2(y[rows, HALF:])
+                s = ss_ref[rows]
+                for u in range(PAIR):
+                    s = s + soft2(y[rows, u * COL_DEV : (u + 1) * COL_DEV])
+                    totals[u] = totals[u] + jnp.exp2(s * slope)
                 ss_ref[rows] = s
-                lower = lower + jnp.exp2(s * slope)
-            upper = jnp.sum(upper, axis=0, keepdims=True)
-            lower = jnp.sum(lower, axis=0, keepdims=True)
-            sw[pl.ds(blk * 16 + i * 2, 1), :] = above - upper
-            sw[pl.ds(blk * 16 + i * 2 + 1, 1), :] = upper - lower
-            above = lower
+            for u in range(PAIR):
+                below = jnp.sum(totals[u], axis=0, keepdims=True)
+                sw[pl.ds(blk * 16 + i * PAIR + u, 1), :] = above - below
+                above = below
         return above
 
     lax.fori_loop(0, 4, block, top)
@@ -170,17 +168,23 @@
     listing_ref, count_ref, zen_ref, lb_ref, sb_ref, flux_ref,
     out,
     fe, f1, f2, te, third16, base, tables, weights,
-    cols, outgoing, arriving, work, mu_send, mu_arrive,
+    cols, cols_pair, work, pick, list_pair, zen_own, zen_pair,
     lw1, lw2, ld, lf, sw1, sw2, sd,
     a1, a2, b1, b2, heads, sw_heads, lw_bias, sw_bias, log_flux, h2, s_ref, e_ref, ss_ref,
-    lw, sw, ret, heat, slab,
+    lw, sw, heat, slab,
     local, w_sem, h_send, h_recv, g_send, g_recv, t_send, t_recv, e_send, e_recv,
-    d_send, d_recv, r_send, r_recv, s_send, s_recv,
+    l_send, l_recv, d_send, d_recv, r_send, r_recv, s_send, s_recv,
 ):
     me, tile = lax.axis_index("group"), lax.axis_index("tile")
     n_tile = lax.axis_size("tile")
     right, left = lax.rem(tile + 1, n_tile), lax.rem(tile + n_tile - 1, n_tile)
-    partner = tile + 1 - 2 * lax.rem(tile, 2)
+    parity = lax.rem(tile, 2)
+    first, last = lax.rem(tile, 32) == 0, (lax.rem(tile, 32) == 31) | (tile == n_tile - 1)
+    others = jnp.logical_not(first)
+    partner = tile + 1 - 2 * parity
+    beyond = lax.rem(tile + n_tile - 1 + 2 * parity, n_tile)
+    early = (lax.rem(lax.div(tile, 2), 4) < 2).astype(jnp.int32)
+    worker = parity == early
     peers = [lax.rem(me + d, N_GROUP) for d in range(1, N_GROUP)]
     levels_of = lambda g: pl.ds(pl.multiple_of(g * 16, 16), 16)
     columns_of = lambda g: pl.ds(pl.multiple_of(g * COL_DEV, COL_DEV), COL_DEV)
@@ -192,10 +196,19 @@
             device_id=where, device_id_type=MESH)
 
     barrier = pltpu.get_barrier_semaphore()
-    for p in (left, right):
-        pl.semaphore_signal(barrier, inc=1, device_id={"tile": p}, device_id_type=MESH)
+
+    def greet(where):
+        pl.semaphore_signal(barrier, inc=1, device_id=where, device_id_type=MESH)
+
+    greet({"tile": partner})
     for p in peers:
-        pl.semaphore_signal(barrier, inc=1, device_id={"group": p}, device_id_type=MESH)
+        greet({"group": p})
+
+    @pl.when(jnp.logical_not(first | last))
+    def _():
+        greet({"tile": beyond})
+
+    zen_own[...] = jnp.broadcast_to(zen_ref[...].astype(f32), (8, COL_DEV))
 
     own = [
         pltpu.make_async_copy(pot, fe.at[:, 3 * HW : 3 * HW + TILE], local.at[0]),
@@ -211,14 +224,20 @@
     ]
     for c in own + stage:
         c.start()
-    pl.semaphore_wait(barrier, N_GROUP + 1)
-
-    halo = [
+    pl.semaphore_wait(barrier, N_GROUP + others.astype(jnp.int32))
+
+    @pl.when(first | last)
+    def _():
+        greet({"tile": beyond})
+
+    to_left = [
         remote(pot.at[:, : 3 * HW], fe.at[:, 3 * HW + TILE :], h_send.at[0], h_recv.at[0], {"tile": left}),
-        remote(pot.at[:, TILE - 3 * HW :], fe.at[:, : 3 * HW], h_send.at[1], h_recv.at[1], {"tile": right}),
-        remote(diff.at[:, : 2 * HW], weights.at[:, 2 * HW + TILE :], h_send.at[2], h_recv.at[2], {"tile": left}),
-        remote(diff.at[:, TILE - 2 * HW :], weights.at[:, : 2 * HW], h_send.at[3], h_recv.at[3], {"tile": right}),
-        remote(nbr.at[:, : 2 * HW], tables.at[:, 2 * HW + TILE :], h_send.at[4], h_recv.at[4], {"tile": left}),
+        remote(diff.at[:, : 2 * HW], weights.at[:, 2 * HW + TILE :], h_send.at[1], h_recv.at[1], {"tile": left}),
+        remote(nbr.at[:, : 2 * HW], tables.at[:, 2 * HW + TILE :], h_send.at[2], h_recv.at[2], {"tile": left}),
+    ]
+    to_right = [
+        remote(pot.at[:, TILE - 3 * HW :], fe.at[:, : 3 * HW], h_send.at[3], h_recv.at[3], {"tile": right}),
+        remote(diff.at[:, TILE - 2 * HW :], weights.at[:, : 2 * HW], h_send.at[4], h_recv.at[4], {"tile": right}),
         remote(nbr.at[:, TILE - 2 * HW :], tables.at[:, : 2 * HW], h_send.at[5], h_recv.at[5], {"tile": right}),
     ]
     gas = [
@@ -226,7 +245,20 @@
                g_send.at[i], g_recv.at[i], {"group": p})
         for i, p in enumerate(peers)
     ]
-    for c in halo + gas:
+    lists = [
+        remote(listing_ref, list_pair, l_send.at[0], l_recv.at[0], {"tile": partner}),
+        remote(zen_own, zen_pair, l_send.at[1], l_recv.at[1], {"tile": partner}),
+    ]
+
+    for c in to_right:
+        c.start()
+
+    @pl.when(others)
+    def _():
+        for c in to_left:
+            c.start()
+
+    for c in lists + gas:
         c.start()
 
     for c in stage:
@@ -241,23 +273,32 @@
     sw_heads[...] = in_two(turned(sd[...]) * LOG2E)
     bias = down(lb_ref[...], 64)
     lw_bias[...] = jnp.concatenate([bias, bias], axis=1)
-    sw_bias[...] = down(sb_ref[...], 64)
-    log_flux[...] = down(jnp.log2(flux_ref[...]), 224)
+    bias = down(sb_ref[...], 64)
+    sw_bias[...] = jnp.concatenate([bias, bias], axis=1)
+    flux = down(jnp.log2(flux_ref[...]), 224)
+    log_flux[...] = jnp.concatenate([flux, flux], axis=1)
     s_ref[...] = jnp.zeros_like(s_ref)
     e_ref[...] = jnp.ones_like(e_ref)
     count = count_ref[...].astype(f32)
     slot = slots_of(listing_ref[...])
-    place = lax.broadcasted_iota(jnp.int32, (COL_DEV, HALF), 1).astype(f32)
-    kept = (slot == place) & (place < count)
-    sent = (slot == place + count - HALF) & (place >= COL_DEV - count)
-    pick = jnp.concatenate([kept.astype(f32), sent.astype(f32)], axis=1).astype(bf16)
-    mu_picked = jnp.dot(
-        jnp.broadcast_to(zen_ref[...], (16, COL_DEV)), pick, preferred_element_type=f32)
-    mu_send[...] = mu_picked[:8, HALF:]
+
+    @pl.when(first)
+    def _():
+        pl.semaphore_wait(barrier, 1)
+        for c in to_left:
+            c.start()
+
+    for c in lists:
+        c.wait()
+    place = lax.broadcasted_iota(jnp.int32, (COL_DEV, COL_DEV), 1).astype(f32)
+    mine = (slot == place) & (place < count)
+    theirs = (slots_of(list_pair[...]) == place - count) & (place >= count)
+    pick[:COL_DEV, :] = mine.astype(f32).astype(bf16)
+    pick[COL_DEV:, :] = theirs.astype(f32).astype(bf16)
 
     for c in own[:3]:
         c.wait()
-    for c in halo:
+    for c in to_left + to_right:
         c.wait()
 
     def put_first(b, at, mid, total):
@@ -294,47 +335,52 @@
     for c in gas + warm:
         c.wait()
 
-    picked = jnp.dot(
-        cols[...].reshape((GAS + 1) * LEV, COL_DEV), pick, preferred_element_type=f32)
-    outgoing[...] = picked[:, HALF:].astype(bf16).reshape(GAS + 1, LEV, HALF)
-    swap = [
-        remote(outgoing, arriving, d_send.at[0], d_recv.at[0], {"tile": partner}),
-        remote(mu_send, mu_arrive, d_send.at[1], d_recv.at[1], {"tile": partner}),
-    ]
-    for c in swap:
-        c.start()
-    work[...] = picked[:, :HALF].astype(bf16).reshape(GAS + 1, LEV, HALF)
-
-    longwave(0, 2, cols, h2, a1, a2, lw_bias, heads, s_ref, e_ref, lw)
-    for c in swap:
-        c.wait()
-    work[...] = work[...] + arriving[...]
-    mu = mu_picked[:1, :HALF] + mu_arrive[:1, :]
-    shortwave(work, h2, b1, b2, sw_bias, sw_heads, log_flux, mu, ss_ref, sw)
-    back = remote(sw, ret, r_send, r_recv, {"tile": partner})
-    back.start()
-    longwave(2, 4, cols, h2, a1, a2, lw_bias, heads, s_ref, e_ref, lw)
-
+    whole = remote(cols, cols_pair, d_send, d_recv, {"tile": partner})
+    back = remote(sw, sw, r_send, r_recv, {"tile": partner})
+
+    @pl.when(jnp.logical_not(worker))
+    def _():
+        whole.start()
+
+    longwave(0, 4, cols, h2, a1, a2, lw_bias, heads, s_ref, e_ref, lw)
+
+    @pl.when(worker)
+    def _():
+        whole.wait_recv()
+        rows = (GAS + 1) * LEV
+        both = jnp.dot(cols[...].reshape(rows, COL_DEV), pick[:COL_DEV, :], preferred_element_type=f32)
+        both = both + jnp.dot(
+            cols_pair[...].reshape(rows, COL_DEV), pick[COL_DEV:, :], preferred_element_type=f32)
+        work[...] = both.astype(bf16).reshape(GAS + 1, LEV, COL_DEV)
+        mu = jnp.dot(zen_own[...].astype(bf16), pick[:COL_DEV, :], preferred_element_type=f32)
+        mu = mu + jnp.dot(zen_pair[...].astype(bf16), pick[COL_DEV:, :], preferred_element_type=f32)
+        shortwave(work, h2, b1, b2, sw_bias, sw_heads, log_flux, mu[:1, :], ss_ref, sw)
+        back.start()
+
+    for c in edges:
+        c.wait()
+    section(te, tables, weights, 4, 6, 14, put_base)
     diag = lax.broadcasted_iota(jnp.int32, (COL_DEV, COL_DEV), 0) == lax.broadcasted_iota(
         jnp.int32, (COL_DEV, COL_DEV), 1)
     slot = jnp.sum(jnp.where(diag, slot, 0.0), axis=0, keepdims=True)
-    here = slot < jnp.minimum(count, HALF)
-    there = (slot >= HALF) & (slot < count)
-    index = jnp.where(there, slot + HALF - count, slot).astype(jnp.int32)
-    index = jnp.bitwise_and(index, HALF - 1)
-    here, there = here.astype(f32), there.astype(f32)
-    back.wait()
+    daylit = (slot < count).astype(f32)
+    first_slot = jnp.where(worker, 0.0, COL_DEV - count)
+    index = jnp.minimum(slot + first_slot, COL_DEV - 1.0).astype(jnp.int32)
+
+    @pl.when(jnp.logical_not(worker))
+    def _():
+        whole.wait_send()
+        back.wait_recv()
+
     planck = jnp.exp(0.25 * cols[0].astype(f32)) * (-(12.0 / 256) * math.log(2.0))
     for half in range(2):
         part = slice(half * HALF, half * HALF + HALF)
-        lane = jnp.broadcast_to(index[:, part], (8, HALF))
+        at = jnp.broadcast_to(index[:, part], (8, HALF))
+        lane, upper = jnp.bitwise_and(at, HALF - 1), at >= HALF
         for r in range(0, LEV, 8):
             rows = slice(r, r + 8)
-            heat[rows, part] = (
-                lw[rows, part] * planck[rows, part]
-                + here[:, part] * taken(sw[rows, :], lane)
-                + there[:, part] * taken(ret[rows, :], lane)
-            )
+            short = jnp.where(upper, taken(sw[rows, HALF:], lane), taken(sw[rows, :HALF], lane))
+            heat[rows, part] = lw[rows, part] * planck[rows, part] + daylit[:, part] * short
     sends = [
         remote(heat.at[levels_of(p), :], slab.at[:, columns], s_send.at[i], s_recv.at[i], {"group": p})
         for i, p in enumerate(peers)
@@ -342,9 +388,11 @@
     for c in sends:
         c.start()
     slab[:, columns] = heat[levels, :]
-    for c in edges:
-        c.wait()
-    section(te, tables, weights, 4, 6, 14, put_base)
+
+    @pl.when(worker)
+    def _():
+        back.wait_send()
+
     for c in sends:
         c.wait()
     out[...] = base[...] + slab[...]
@@ -371,17 +419,17 @@
             at32(16, WIDE), at32(16, WIDE), at32(16, WIDE), at32(16, TILE + 2 * HW),
             at16(16, TILE), at32(16, TILE),
             pltpu.VMEM((NB, TABLE), jnp.int32), at32(NB, TABLE),
-            at16(8, LEV, COL_DEV), at16(8, LEV, HALF), at16(8, LEV, HALF), at16(8, LEV, HALF),
-            at32(8, HALF), at32(8, HALF),
+            at16(8, LEV, COL_DEV), at16(8, LEV, COL_DEV), at16(8, LEV, COL_DEV),
+            at16(2 * COL_DEV, COL_DEV), pltpu.VMEM((1, COL_DEV), jnp.int32), at32(8, COL_DEV), at32(8, COL_DEV),
             at16(8, 64), at16(64, 64), at16(64, 256), at16(64, 256),
             at16(8, 64), at16(64, 64), at16(64, 224),
             at16(1024, 128), at16(128, 128), at16(1024, 128), at16(128, 128),
             at16(512, 128), at16(224, 128),
-            at32(64, COL_DEV), at32(64, HALF), at32(224, HALF),
-            at16(1024, COL_DEV), at32(256, COL_DEV), at32(256, COL_DEV), at32(224, HALF),
-            at32(LEV, COL_DEV), at32(LEV, HALF), at32(LEV, HALF), at32(LEV, COL_DEV), at32(16, TILE),
+            at32(64, COL_DEV), at32(64, COL_DEV), at32(224, COL_DEV),
+            at16(1024, COL_DEV), at32(256, COL_DEV), at32(256, COL_DEV), at32(224, COL_DEV),
+            at32(LEV, COL_DEV), at32(LEV, COL_DEV), at32(LEV, COL_DEV), at32(16, TILE),
             dma((4,)), dma((7,)), dma((6,)), dma((6,)), dma((3,)), dma((3,)), dma((3,)), dma((3,)),
-            dma((2,)), dma((2,)), dma((2,)), dma((2,)), dma(()), dma(()), dma((3,)), dma((3,)),
+            dma((2,)), dma((2,)), dma((2,)), dma((2,)), dma(()), dma(()), dma(()), dma(()), dma((3,)), dma((3,)),
         ],
         compiler_params=pltpu.CompilerParams(
             collective_id=0, has_side_effects=True, vmem_limit_bytes=60 * 2**20),

time: 52.5 us -> 48.7 us (0.928)
  Pallas kernels: 50.2 us -> 46.4 us
    pallas_call x1, Pallas kernels: 50.2 us -> 46.4 us  [per_device(): pl.pallas_call(kernel, out_shape=jax.ShapeDtypeStruct((16, TILE), f32), i...]
where the time goes in v3:
time: 48.7 us; the launch traced here: 48.5 us
  Pallas kernels  46.4 us (95%)
  local copies, waits for them, and re-layouts  1.47 us (3%)
  between operations  0.66 us (1%)
    pallas_call x1, Pallas kernels, per_device(): pl.pallas_call(kernel, out_shape=jax.ShapeDtypeStruct((16, TILE), f32), i...  46.4 us
    unnamed x1, local copies, waits for them, and re-layouts  1.47 us

profile of v3, /device:TPU:32, one launch (start us, length us, event | category | flops | bytes accessed | tf_op | source)
XLA Modules:
  0.0 48.5 jit_solution(10427213609380866896)
XLA Ops:
  0.7 46.4 %step.1 = f32[16,1024]{1,0:T(8,128)} custom-call(f32[16,1024]{1,0:T(8,128)} %pot.1, bf16[7,16,1024]{2,1,0:T(8,128)(2,1)} %species.1, f32[4,1024]{1,0:T(4,128)} %diff.1, s32[4,1024]{1,0:T(4,128)} %nbr.1, bf16[8,64]{1,0:T(8,128)(2,1)} %lw1_h.1, bf16[64,64]{1,0:T(8,128)(2,1)} %lw2_h.1, bf16[64,256]{1,0:T(8,128)(2,1)} %ld_h.1, bf16[64,256]{1,0:T(8,128)(2,1)} %lf_h.1, ...), custom_call_target="tpu_custom_call" | custom-call | tf_op jit(solution)/shard_map/step/pallas_call | solution.py:413
  47.0 1.5 %copy.20 = f32[16,1024]{1,0:T(8,128)} copy(f32[16,1024]{1,0:T(8,128)} %step.1) | data formatting | bytes 131072

commit v4 on v3

--- a/solution.py
+++ b/solution.py
@@ -73,8 +73,8 @@
         h2[q * 128 : (q + 1) * 128, :width] = two.astype(bf16)
 
 
-def longwave(lo, hi, cols, h2, a1, a2, bias, heads, s_ref, e_ref, lw):
-    @pl.loop(lo, hi)
+def longwave(cols, h2, a1, a2, bias, heads, s_ref, e_ref, lw, hand_on):
+    @pl.loop(0, N_GROUP)
     def _(blk):
         hidden(h2, cols, a1, a2, bias[...], COL_DEV, blk)
         for i in range(16 // PAIR):
@@ -96,10 +96,13 @@
                 s_ref[rows] = s
                 e_ref[rows] = above
             for u in range(PAIR):
-                lw[pl.ds(blk * 16 + i * PAIR + u, 1), :] = jnp.sum(totals[u], axis=0, keepdims=True)
-
-
-def shortwave(work, h2, b1, b2, bias, heads, log_flux, mu, ss_ref, sw):
+                lw[i * PAIR + u : i * PAIR + u + 1, :] = jnp.sum(totals[u], axis=0, keepdims=True)
+        levels = pl.ds(pl.multiple_of(blk * 16, 16), 16)
+        planck = jnp.exp(0.25 * cols[0, levels, :].astype(f32)) * (-(12.0 / 256) * math.log(2.0))
+        hand_on(blk, levels, lw[...] * planck)
+
+
+def shortwave(work, h2, b1, b2, bias, heads, log_flux, mu, ss_ref, sw, hand_on):
     slope = jnp.broadcast_to(-0.1 / mu, (8, COL_DEV))
     ss_ref[...] = jnp.broadcast_to(-10.0 * mu, (224, COL_DEV)) * log_flux[...]
     top = jnp.sum(jnp.exp2(log_flux[...]), axis=0, keepdims=True)
@@ -120,12 +123,12 @@
                 ss_ref[rows] = s
             for u in range(PAIR):
                 below = jnp.sum(totals[u], axis=0, keepdims=True)
-                sw[pl.ds(blk * 16 + i * PAIR + u, 1), :] = above - below
+                sw[i * PAIR + u : i * PAIR + u + 1, :] = above - below
                 above = below
+        hand_on(blk, pl.ds(pl.multiple_of(blk * 16, 16), 16), sw[...] * (mu * (12.0 / 224)))
         return above
 
-    lax.fori_loop(0, 4, block, top)
-    sw[...] = sw[...] * (mu * (12.0 / 224))
+    lax.fori_loop(0, N_GROUP, block, top)
 
 
 def section(src, tables, weights, src_shift, lo, hi, put):
@@ -150,7 +153,7 @@
         put(b, at, mid, total)
         return c
 
-    lax.fori_loop(lo, hi, step, 0, unroll=4)
+    lax.fori_loop(lo, hi, step, 0, unroll=hi - lo)
 
 
 def taken(rows, lane):
@@ -165,15 +168,15 @@
 
 def kernel(
     pot, species, diff, nbr, lw1_h, lw2_h, ld_h, lf_h, sw1_h, sw2_h, sd_h,
-    listing_ref, count_ref, zen_ref, lb_ref, sb_ref, flux_ref,
+    listing_h, count_h, zen_h, lb_h, sb_h, flux_h,
     out,
     fe, f1, f2, te, third16, base, tables, weights,
     cols, cols_pair, work, pick, list_pair, zen_own, zen_pair,
-    lw1, lw2, ld, lf, sw1, sw2, sd,
+    lw1, lw2, ld, lf, sw1, sw2, sd, listing_ref, count_ref, zen_ref, lb_ref, sb_ref, flux_ref,
     a1, a2, b1, b2, heads, sw_heads, lw_bias, sw_bias, log_flux, h2, s_ref, e_ref, ss_ref,
-    lw, sw, heat, slab,
+    lw, sw, heat, short_own, short_pair, slab, short_slab,
     local, w_sem, h_send, h_recv, g_send, g_recv, t_send, t_recv, e_send, e_recv,
-    l_send, l_recv, d_send, d_recv, r_send, r_recv, s_send, s_recv,
+    l_send, l_recv, d_send, d_recv, s_send, s_recv, o_send, o_recv, p_send,
 ):
     me, tile = lax.axis_index("group"), lax.axis_index("tile")
     n_tile = lax.axis_size("tile")
@@ -203,12 +206,11 @@
     greet({"tile": partner})
     for p in peers:
         greet({"group": p})
+        greet({"group": p, "tile": partner})
 
     @pl.when(jnp.logical_not(first | last))
     def _():
         greet({"tile": beyond})
-
-    zen_own[...] = jnp.broadcast_to(zen_ref[...].astype(f32), (8, COL_DEV))
 
     own = [
         pltpu.make_async_copy(pot, fe.at[:, 3 * HW : 3 * HW + TILE], local.at[0]),
@@ -220,11 +222,16 @@
     stage = [
         pltpu.make_async_copy(src, dst, w_sem.at[i])
         for i, (src, dst) in enumerate(
-            [(lw1_h, lw1), (lw2_h, lw2), (ld_h, ld), (lf_h, lf), (sw1_h, sw1), (sw2_h, sw2), (sd_h, sd)])
+            [(lw1_h, lw1), (lw2_h, lw2), (ld_h, ld), (lf_h, lf), (sw1_h, sw1), (sw2_h, sw2), (sd_h, sd),
+             (lb_h, lb_ref), (sb_h, sb_ref), (flux_h, flux_ref),
+             (listing_h, listing_ref), (count_h, count_ref), (zen_h, zen_ref)])
     ]
     for c in own + stage:
         c.start()
-    pl.semaphore_wait(barrier, N_GROUP + others.astype(jnp.int32))
+    for c in stage:
+        c.wait()
+    zen_own[...] = jnp.broadcast_to(zen_ref[...].astype(f32), (8, COL_DEV))
+    pl.semaphore_wait(barrier, 2 * N_GROUP - 1 + others.astype(jnp.int32))
 
     @pl.when(first | last)
     def _():
@@ -261,8 +268,6 @@
     for c in lists + gas:
         c.start()
 
-    for c in stage:
-        c.wait()
     spread_first(a1, lw1)
     spread_first(b1, sw1)
     two_blocks(a2, lw2)
@@ -290,11 +295,13 @@
 
     for c in lists:
         c.wait()
+    pair_slot = slots_of(list_pair[...]) + count
     place = lax.broadcasted_iota(jnp.int32, (COL_DEV, COL_DEV), 1).astype(f32)
-    mine = (slot == place) & (place < count)
-    theirs = (slots_of(list_pair[...]) == place - count) & (place >= count)
-    pick[:COL_DEV, :] = mine.astype(f32).astype(bf16)
-    pick[COL_DEV:, :] = theirs.astype(f32).astype(bf16)
+    column = lax.broadcasted_iota(jnp.int32, (COL_DEV, COL_DEV), 0).astype(f32)
+    pick[:COL_DEV, :] = ((slot == place) & (place < count)).astype(f32).astype(bf16)
+    pick[COL_DEV:, :] = ((pair_slot == place) & (place >= count)).astype(f32).astype(bf16)
+    across = lambda v: jnp.sum(jnp.where(column == place, v, 0.0), axis=0, keepdims=True)
+    slot, pair_slot = across(slot), across(pair_slot)
 
     for c in own[:3]:
         c.wait()
@@ -336,13 +343,55 @@
         c.wait()
 
     whole = remote(cols, cols_pair, d_send, d_recv, {"tile": partner})
-    back = remote(sw, sw, r_send, r_recv, {"tile": partner})
 
     @pl.when(jnp.logical_not(worker))
     def _():
         whole.start()
 
-    longwave(0, 4, cols, h2, a1, a2, lw_bias, heads, s_ref, e_ref, lw)
+    def hand_long(blk, rows, value):
+        d = lax.rem(blk - me + N_GROUP, N_GROUP)
+        heat[rows, :] = value
+
+        @pl.when(d == 0)
+        def _():
+            slab[:, columns] = value
+
+        @pl.when(d > 0)
+        def _():
+            remote(heat.at[rows, :], slab.at[:, columns], s_send.at[d], s_recv.at[d], {"group": blk}).start()
+
+    def hand_short(blk, rows, value):
+        def placed(at, lit, half):
+            part = slice(half * HALF, half * HALF + HALF)
+            at = jnp.broadcast_to(at[:, part], (8, HALF))
+            lane, upper = jnp.bitwise_and(at, HALF - 1), at >= HALF
+            both = [
+                jnp.where(upper, taken(value[r : r + 8, HALF:], lane), taken(value[r : r + 8, :HALF], lane))
+                for r in (0, 8)
+            ]
+            return jnp.concatenate(both, axis=0) * lit[:, part]
+
+        limit = lambda v: jnp.minimum(v, COL_DEV - 1.0).astype(jnp.int32)
+        own_at, pair_at = limit(slot), limit(pair_slot)
+        own_lit, pair_lit = (slot < count).astype(f32), (pair_slot < COL_DEV).astype(f32)
+        mine = jnp.concatenate([placed(own_at, own_lit, h) for h in range(2)], axis=1)
+        short_own[rows, :] = mine
+        short_pair[rows, :] = jnp.concatenate([placed(pair_at, pair_lit, h) for h in range(2)], axis=1)
+        d = lax.rem(blk - me + N_GROUP, N_GROUP)
+
+        @pl.when(d == 0)
+        def _():
+            short_slab[:, columns] = mine
+
+        @pl.when(d > 0)
+        def _():
+            remote(short_own.at[rows, :], short_slab.at[:, columns], o_send.at[d], o_recv.at[d],
+                   {"group": blk}).start()
+
+        remote(short_pair.at[rows, :], short_slab.at[:, columns], p_send.at[d], o_recv.at[d],
+               {"group": blk, "tile": partner}).start()
+
+    longwave(cols, h2, a1, a2, lw_bias, heads, s_ref, e_ref, lw, hand_long)
 
     @pl.when(worker)
     def _():
@@ -354,48 +403,34 @@
         work[...] = both.astype(bf16).reshape(GAS + 1, LEV, COL_DEV)
         mu = jnp.dot(zen_own[...].astype(bf16), pick[:COL_DEV, :], preferred_element_type=f32)
         mu = mu + jnp.dot(zen_pair[...].astype(bf16), pick[COL_DEV:, :], preferred_element_type=f32)
-        shortwave(work, h2, b1, b2, sw_bias, sw_heads, log_flux, mu[:1, :], ss_ref, sw)
-        back.start()
+        shortwave(work, h2, b1, b2, sw_bias, sw_heads, log_flux, mu[:1, :], ss_ref, sw, hand_short)
 
     for c in edges:
         c.wait()
     section(te, tables, weights, 4, 6, 14, put_base)
-    diag = lax.broadcasted_iota(jnp.int32, (COL_DEV, COL_DEV), 0) == lax.broadcasted_iota(
-        jnp.int32, (COL_DEV, COL_DEV), 1)
-    slot = jnp.sum(jnp.where(diag, slot, 0.0), axis=0, keepdims=True)
-    daylit = (slot < count).astype(f32)
-    first_slot = jnp.where(worker, 0.0, COL_DEV - count)
-    index = jnp.minimum(slot + first_slot, COL_DEV - 1.0).astype(jnp.int32)
+
+    def sent(src, dst, send, recv):
+        return remote(src.at[:16, :], dst.at[:, columns], send, recv, {"group": peers[0]})
+
+    for d in range(1, N_GROUP):
+        c = sent(heat, slab, s_send.at[d], s_recv.at[d])
+        c.wait_send()
+        c.wait_recv()
+        sent(short_own, short_slab, o_send.at[d], o_recv.at[d]).wait_recv()
+
+    @pl.when(worker)
+    def _():
+        for d in range(N_GROUP):
+            sent(short_pair, short_slab, p_send.at[d], o_recv.at[d]).wait_send()
+        for d in range(1, N_GROUP):
+            sent(short_own, short_slab, o_send.at[d], o_recv.at[d]).wait_send()
 
     @pl.when(jnp.logical_not(worker))
     def _():
         whole.wait_send()
-        back.wait_recv()
-
-    planck = jnp.exp(0.25 * cols[0].astype(f32)) * (-(12.0 / 256) * math.log(2.0))
-    for half in range(2):
-        part = slice(half * HALF, half * HALF + HALF)
-        at = jnp.broadcast_to(index[:, part], (8, HALF))
-        lane, upper = jnp.bitwise_and(at, HALF - 1), at >= HALF
-        for r in range(0, LEV, 8):
-            rows = slice(r, r + 8)
-            short = jnp.where(upper, taken(sw[rows, HALF:], lane), taken(sw[rows, :HALF], lane))
-            heat[rows, part] = lw[rows, part] * planck[rows, part] + daylit[:, part] * short
-    sends = [
-        remote(heat.at[levels_of(p), :], slab.at[:, columns], s_send.at[i], s_recv.at[i], {"group": p})
-        for i, p in enumerate(peers)
-    ]
-    for c in sends:
-        c.start()
-    slab[:, columns] = heat[levels, :]
-
-    @pl.when(worker)
-    def _():
-        back.wait_send()
-
-    for c in sends:
-        c.wait()
-    out[...] = base[...] + slab[...]
+        sent(short_own, short_slab, o_send.at[0], o_recv.at[0]).wait_recv()
+
+    out[...] = base[...] + slab[...] + short_slab[...]
 
 
 VMEM = pl.BlockSpec(memory_space=pltpu.VMEM)
@@ -413,7 +448,7 @@
     return pl.pallas_call(
         kernel,
         out_shape=jax.ShapeDtypeStruct((16, TILE), f32),
-        in_specs=[ANY] * 11 + [VMEM] * 6,
+        in_specs=[ANY] * 17,
         out_specs=VMEM,
         scratch_shapes=[
             at32(16, WIDE), at32(16, WIDE), at32(16, WIDE), at32(16, TILE + 2 * HW),
@@ -423,13 +458,17 @@
             at16(2 * COL_DEV, COL_DEV), pltpu.VMEM((1, COL_DEV), jnp.int32), at32(8, COL_DEV), at32(8, COL_DEV),
             at16(8, 64), at16(64, 64), at16(64, 256), at16(64, 256),
             at16(8, 64), at16(64, 64), at16(64, 224),
+            pltpu.VMEM((1, COL_DEV), jnp.int32), pltpu.VMEM((1, 1), jnp.int32), at16(1, COL_DEV),
+            at32(1, 64), at32(1, 64), at32(1, 224),
             at16(1024, 128), at16(128, 128), at16(1024, 128), at16(128, 128),
             at16(512, 128), at16(224, 128),
             at32(64, COL_DEV), at32(64, COL_DEV), at32(224, COL_DEV),
             at16(1024, COL_DEV), at32(256, COL_DEV), at32(256, COL_DEV), at32(224, COL_DEV),
-            at32(LEV, COL_DEV), at32(LEV, COL_DEV), at32(LEV, COL_DEV), at32(16, TILE),
-            dma((4,)), dma((7,)), dma((6,)), dma((6,)), dma((3,)), dma((3,)), dma((3,)), dma((3,)),
-            dma((2,)), dma((2,)), dma((2,)), dma((2,)), dma(()), dma(()), dma(()), dma(()), dma((3,)), dma((3,)),
+            at32(16, COL_DEV), at32(16, COL_DEV), at32(LEV, COL_DEV), at32(LEV, COL_DEV), at32(LEV, COL_DEV),
+            at32(16, TILE), at32(16, TILE),
+            dma((4,)), dma((13,)), dma((6,)), dma((6,)), dma((3,)), dma((3,)), dma((3,)), dma((3,)),
+            dma((2,)), dma((2,)), dma((2,)), dma((2,)), dma(()), dma(()),
+            dma((4,)), dma((4,)), dma((4,)), dma((4,)), dma((4,)),
         ],
         compiler_params=pltpu.CompilerParams(
             collective_id=0, has_side_effects=True, vmem_limit_bytes=60 * 2**20),

time: 48.7 us -> 45.8 us (0.940)
  the two profiles are of different devices: /device:TPU:32 before, /device:TPU:96 now
where the time goes in v4:
time: 45.8 us; the launch traced here: 45.6 us
  Pallas kernels  43.5 us (95%)
  local copies, waits for them, and re-layouts  1.47 us (3%)
  between operations  0.66 us (1%)
    pallas_call x1, Pallas kernels, per_device(): pl.pallas_call(kernel, out_shape=jax.ShapeDtypeStruct((16, TILE), f32), i...  43.5 us
    unnamed x1, local copies, waits for them, and re-layouts  1.47 us

profile of v4, /device:TPU:96, one launch (start us, length us, event | category | flops | bytes accessed | tf_op | source)
XLA Modules:
  0.0 45.6 jit_solution(2725810933105186278)
XLA Ops:
  0.7 43.5 %step.1 = f32[16,1024]{1,0:T(8,128)} custom-call(f32[16,1024]{1,0:T(8,128)} %pot.1, bf16[7,16,1024]{2,1,0:T(8,128)(2,1)} %species.1, f32[4,1024]{1,0:T(4,128)} %diff.1, s32[4,1024]{1,0:T(4,128)} %nbr.1, bf16[8,64]{1,0:T(8,128)(2,1)} %lw1_h.1, bf16[64,64]{1,0:T(8,128)(2,1)} %lw2_h.1, bf16[64,256]{1,0:T(8,128)(2,1)} %ld_h.1, bf16[64,256]{1,0:T(8,128)(2,1)} %lf_h.1, ...), custom_call_target="tpu_custom_call" | custom-call | tf_op jit(solution)/shard_map/step/pallas_call | solution.py:448
  44.1 1.5 %copy.20 = f32[16,1024]{1,0:T(8,128)} copy(f32[16,1024]{1,0:T(8,128)} %step.1) | data formatting | bytes 131072

commit v5 on v4

--- a/solution.py
+++ b/solution.py
@@ -73,9 +73,10 @@
         h2[q * 128 : (q + 1) * 128, :width] = two.astype(bf16)
 
 
-def longwave(cols, h2, a1, a2, bias, heads, s_ref, e_ref, lw, hand_on):
+def longwave(cols, h2, a1, a2, bias, heads, s_ref, e_ref, lw, arrived, hand_on):
     @pl.loop(0, N_GROUP)
     def _(blk):
+        arrived(blk)
         hidden(h2, cols, a1, a2, bias[...], COL_DEV, blk)
         for i in range(16 // PAIR):
             h = jnp.concatenate(
@@ -177,6 +178,7 @@
     lw, sw, heat, short_own, short_pair, slab, short_slab,
     local, w_sem, h_send, h_recv, g_send, g_recv, t_send, t_recv, e_send, e_recv,
     l_send, l_recv, d_send, d_recv, s_send, s_recv, o_send, o_recv, p_send,
+    x_send, x_recv,
 ):
     me, tile = lax.axis_index("group"), lax.axis_index("tile")
     n_tile = lax.axis_size("tile")
@@ -335,18 +337,38 @@
         remote(te.at[:, HW : 2 * HW], te.at[:, HW + TILE :], e_send.at[0], e_recv.at[0], {"tile": left}),
         remote(te.at[:, TILE : HW + TILE], te.at[:, :HW], e_send.at[1], e_recv.at[1], {"tile": right}),
     ]
-    for c in warm + edges:
+    warm_pair = [
+        remote(third16.at[:, columns_of(p)], cols_pair.at[0, levels, :],
+               x_send.at[i], x_recv.at[i], {"group": p, "tile": partner})
+        for i, p in enumerate([me] + peers)
+    ]
+    for c in warm:
+        c.start()
+
+    @pl.when(jnp.logical_not(worker))
+    def _():
+        for c in warm_pair:
+            c.start()
+
+    for c in edges:
         c.start()
     cols[0, levels, :] = third16[:, columns]
     own[3].wait()
-    for c in gas + warm:
+    for c in gas:
         c.wait()
-
-    whole = remote(cols, cols_pair, d_send, d_recv, {"tile": partner})
+    whole = remote(cols.at[1:], cols_pair.at[1:], d_send, d_recv, {"tile": partner})
 
     @pl.when(jnp.logical_not(worker))
     def _():
         whole.start()
+
+    def arrived(blk):
+        d = lax.rem(me - blk + N_GROUP, N_GROUP)
+
+        @pl.when(d > 0)
+        def _():
+            remote(third16.at[:, columns], cols.at[0, levels, :], t_send.at[d - 1], t_recv.at[d - 1],
+                   {"group": peers[0]}).wait_recv()
 
     def hand_long(blk, rows, value):
         d = lax.rem(blk - me + N_GROUP, N_GROUP)
@@ -391,11 +413,13 @@
         remote(short_pair.at[rows, :], short_slab.at[:, columns], p_send.at[d], o_recv.at[d],
                {"group": blk, "tile": partner}).start()
 
-    longwave(cols, h2, a1, a2, lw_bias, heads, s_ref, e_ref, lw, hand_long)
+    longwave(cols, h2, a1, a2, lw_bias, heads, s_ref, e_ref, lw, arrived, hand_long)
 
     @pl.when(worker)
     def _():
         whole.wait_recv()
+        for c in warm_pair:
+            c.wait_recv()
         rows = (GAS + 1) * LEV
         both = jnp.dot(cols[...].reshape(rows, COL_DEV), pick[:COL_DEV, :], preferred_element_type=f32)
         both = both + jnp.dot(
@@ -408,6 +432,8 @@
     for c in edges:
         c.wait()
     section(te, tables, weights, 4, 6, 14, put_base)
+    for c in warm:
+        c.wait_send()
 
     def sent(src, dst, send, recv):
         return remote(src.at[:16, :], dst.at[:, columns], send, recv, {"group": peers[0]})
@@ -428,6 +454,8 @@
     @pl.when(jnp.logical_not(worker))
     def _():
         whole.wait_send()
+        for c in warm_pair:
+            c.wait_send()
         sent(short_own, short_slab, o_send.at[0], o_recv.at[0]).wait_recv()
 
     out[...] = base[...] + slab[...] + short_slab[...]
@@ -468,7 +496,7 @@
             at32(16, TILE), at32(16, TILE),
             dma((4,)), dma((13,)), dma((6,)), dma((6,)), dma((3,)), dma((3,)), dma((3,)), dma((3,)),
             dma((2,)), dma((2,)), dma((2,)), dma((2,)), dma(()), dma(()),
-            dma((4,)), dma((4,)), dma((4,)), dma((4,)), dma((4,)),
+            dma((4,)), dma((4,)), dma((4,)), dma((4,)), dma((4,)), dma((4,)), dma((4,)),
         ],
         compiler_params=pltpu.CompilerParams(
             collective_id=0, has_side_effects=True, vmem_limit_bytes=60 * 2**20),

time: 45.8 us -> 44.5 us (0.972)
  Pallas kernels: 43.5 us -> 42.2 us
    pallas_call x1, Pallas kernels: 43.5 us -> 42.2 us  [per_device(): pl.pallas_call(kernel, out_shape=jax.ShapeDtypeStruct((16, TILE), f32), i...]
where the time goes in v5:
time: 44.5 us; the launch traced here: 44.3 us
  Pallas kernels  42.2 us (95%)
  local copies, waits for them, and re-layouts  1.47 us (3%)
  between operations  0.66 us (1%)
    pallas_call x1, Pallas kernels, per_device(): pl.pallas_call(kernel, out_shape=jax.ShapeDtypeStruct((16, TILE), f32), i...  42.2 us
    unnamed x1, local copies, waits for them, and re-layouts  1.47 us

profile of v5, /device:TPU:96, one launch (start us, length us, event | category | flops | bytes accessed | tf_op | source)
XLA Modules:
  0.0 44.3 jit_solution(11570850892833246166)
XLA Ops:
  0.7 42.2 %step.1 = f32[16,1024]{1,0:T(8,128)} custom-call(f32[16,1024]{1,0:T(8,128)} %pot.1, bf16[7,16,1024]{2,1,0:T(8,128)(2,1)} %species.1, f32[4,1024]{1,0:T(4,128)} %diff.1, s32[4,1024]{1,0:T(4,128)} %nbr.1, bf16[8,64]{1,0:T(8,128)(2,1)} %lw1_h.1, bf16[64,64]{1,0:T(8,128)(2,1)} %lw2_h.1, bf16[64,256]{1,0:T(8,128)(2,1)} %ld_h.1, bf16[64,256]{1,0:T(8,128)(2,1)} %lf_h.1, ...), custom_call_target="tpu_custom_call" | custom-call | tf_op jit(solution)/shard_map/step/pallas_call | solution.py:476
  42.8 1.5 %copy.20 = f32[16,1024]{1,0:T(8,128)} copy(f32[16,1024]{1,0:T(8,128)} %step.1) | data formatting | bytes 131072

commit v6 on v5

--- a/solution.py
+++ b/solution.py
@@ -296,7 +296,7 @@
             c.start()
 
     for c in lists:
-        c.wait()
+        c.wait_recv()
     pair_slot = slots_of(list_pair[...]) + count
     place = lax.broadcasted_iota(jnp.int32, (COL_DEV, COL_DEV), 1).astype(f32)
     column = lax.broadcasted_iota(jnp.int32, (COL_DEV, COL_DEV), 0).astype(f32)
@@ -308,7 +308,7 @@
     for c in own[:3]:
         c.wait()
     for c in to_left + to_right:
-        c.wait()
+        c.wait_recv()
 
     def put_first(b, at, mid, total):
         f1[:, at(b)] = mid + total
@@ -355,7 +355,7 @@
     cols[0, levels, :] = third16[:, columns]
     own[3].wait()
     for c in gas:
-        c.wait()
+        c.wait_recv()
     whole = remote(cols.at[1:], cols_pair.at[1:], d_send, d_recv, {"tile": partner})
 
     @pl.when(jnp.logical_not(worker))
@@ -430,9 +430,9 @@
         shortwave(work, h2, b1, b2, sw_bias, sw_heads, log_flux, mu[:1, :], ss_ref, sw, hand_short)
 
     for c in edges:
-        c.wait()
+        c.wait_recv()
     section(te, tables, weights, 4, 6, 14, put_base)
-    for c in warm:
+    for c in to_left + to_right + lists + gas + warm + edges:
         c.wait_send()
 
     def sent(src, dst, send, recv):

time: 44.5 us -> 42.7 us (0.960)
  the two profiles are of different devices: /device:TPU:96 before, /device:TPU:1 now
where the time goes in v6:
time: 42.7 us; the launch traced here: 42.5 us
  Pallas kernels  40.4 us (95%)
  local copies, waits for them, and re-layouts  1.47 us (3%)
  between operations  0.66 us (2%)
    pallas_call x1, Pallas kernels, per_device(): pl.pallas_call(kernel, out_shape=jax.ShapeDtypeStruct((16, TILE), f32), i...  40.4 us
    unnamed x1, local copies, waits for them, and re-layouts  1.47 us

profile of v6, /device:TPU:1, one launch (start us, length us, event | category | flops | bytes accessed | tf_op | source)
XLA Modules:
  0.0 42.5 jit_solution(7792021981710058326)
XLA Ops:
  0.7 40.4 %step.1 = f32[16,1024]{1,0:T(8,128)} custom-call(f32[16,1024]{1,0:T(8,128)} %pot.1, bf16[7,16,1024]{2,1,0:T(8,128)(2,1)} %species.1, f32[4,1024]{1,0:T(4,128)} %diff.1, s32[4,1024]{1,0:T(4,128)} %nbr.1, bf16[8,64]{1,0:T(8,128)(2,1)} %lw1_h.1, bf16[64,64]{1,0:T(8,128)(2,1)} %lw2_h.1, bf16[64,256]{1,0:T(8,128)(2,1)} %ld_h.1, bf16[64,256]{1,0:T(8,128)(2,1)} %lf_h.1, ...), custom_call_target="tpu_custom_call" | custom-call | tf_op jit(solution)/shard_map/step/pallas_call | solution.py:476
  41.0 1.5 %copy.20 = f32[16,1024]{1,0:T(8,128)} copy(f32[16,1024]{1,0:T(8,128)} %step.1) | data formatting | bytes 131072
